TPU v7x, 32 devices: a whole 2x2x4 slice. The times are simulated.
32 devices in a mesh: expert: 8 (over z, x), dp: 4 (over y, core).
Axes of the slice: x: 2, y: 2, z: 4, core: 2. Of those that a mesh axis runs over, the one named last changes fastest.
Arguments:
- features: bfloat16 [4096, 32, 64], P(('expert', 'dp')), may hold values from -1 to 1
- spacing: float32 [4096, 32], P(('expert', 'dp')), may hold values from 0.02 to 0.3
- targets: float32 [3, 4096], P(None, ('expert', 'dp')), may hold values from 0 to 1
- ray_length: int32 [4096], P(('expert', 'dp')), may hold values from 1 to 32, as said below
- cell_id: int32 [4096, 32], P(('expert', 'dp')), may hold values from 0 to 15, as said below
- slot_rank: int32 [4096, 32], P(('expert', 'dp')), may hold values from -1 to 383, as said below
- image_id: int32 [4096], P(('expert', 'dp')), may hold values from 0 to 511, as said below
- params: float32 [16, 848, 256], P('expert'), may hold values from -5 to 5
- first_moment: float32 [16, 848, 256], P('expert'), may hold values from -0.75 to 0.75
- second_moment: float32 [16, 848, 256], P('expert'), may hold values from 1e-06 to 0.01
- code_table: float32 [512, 64], P(('expert', 'dp')), may hold values from -6 to 6
- table_first: float32 [512, 64], P(('expert', 'dp')), may hold values from -0.75 to 0.75
- table_second: float32 [512, 64], P(('expert', 'dp')), may hold values from 1e-06 to 0.01
Outputs:
- ray_loss: float32 [4096], P(('expert', 'dp'))
- new_params: float32 [16, 848, 256], P('expert')
- new_first_moment: float32 [16, 848, 256], P('expert')
- new_second_moment: float32 [16, 848, 256], P('expert')
- new_code_table: float32 [512, 64], P(('expert', 'dp'))
- new_table_first: float32 [512, 64], P(('expert', 'dp'))
- new_table_second: float32 [512, 64], P(('expert', 'dp'))
Inputs may be any that keep to these rules, and one draw needn't show every extreme that they name: `ray_length`: rays form aligned blocks of 128, one a device, in the order of the axes expert then dp. In every block the lengths sum to 3072 and some ray has all 32 samples. `cell_id`: also given for samples at or beyond their ray's length, where it is unused. `slot_rank`: for a sample below its ray's length: its rank among the live samples of its block of 128 rays that have the same cell_id, counted ray by ray and along each ray; -1 for the other samples. No block has more than 384 live samples of one cell_id; in every block some cell_id has exactly 384, and one cell_id has 384 in every block. `image_id`: A ray of block b names an image from b * 16 to (b + 1) * 16 - 1.
All inputs are finite; a program needn't handle non-finite values.
Results may differ from a plain program's by a relative error of at most 0.0046.
Values may be sent and summed in bfloat16 or wider, within the bound.
A program may use at most 128 MiB of HBM per device.

v0:
```python
import functools

import jax
import jax.numpy as jnp
from jax import lax
from jax.experimental import pallas as pl
from jax.experimental.pallas import tpu as pltpu
from jax.sharding import PartitionSpec as P

NET_WIDTH = 256
CODE_WIDTH = 64
ENC_WIDTH = 64
LAYERS = 4
SAMPLES = 32
HEAD_ROW = ENC_WIDTH + (LAYERS - 1) * NET_WIDTH
LANES = 128

BETA_ONE = 0.9
BETA_TWO = 0.999
LEARN_RATE = 0.001
ADAM_EPS = 1e-08
CORRECT_ONE = 1.0 - 0.9**10
CORRECT_TWO = 1.0 - 0.999**10

MESH = pl.DeviceIdType.MESH
VMEM = pl.BlockSpec(memory_space=pltpu.VMEM)
SMEM = pl.BlockSpec(memory_space=pltpu.SMEM)
F32 = jnp.float32
BF16 = jnp.bfloat16
NN = (((1,), (0,)), ((), ()))
NT = (((1,), (1,)), ((), ()))
TN = (((0,), (0,)), ((), ()))


def dot(left, right, dims=NN, precision=None):
    return lax.dot_general(left, right, dims, precision=precision, preferred_element_type=F32)


def exact(left, right, dims=NN):
    return dot(left, right, dims, lax.Precision.HIGHEST)


def adam_update(param_now, gradient, moment_one, moment_two):
    new_one = BETA_ONE * moment_one + (1.0 - BETA_ONE) * gradient
    new_two = BETA_TWO * moment_two + (1.0 - BETA_TWO) * gradient * gradient
    update = LEARN_RATE * (new_one / CORRECT_ONE) / (jnp.sqrt(new_two / CORRECT_TWO) + ADAM_EPS)
    return (param_now - update, new_one, new_two)


def lane_block(index):
    return pl.ds(pl.multiple_of(index * LANES, LANES), LANES)


def move_rows(count, move):
    step = 128

    def body(block, carry):
        for inner in range(step):
            move(block * step + inner)
        return carry

    lax.fori_loop(0, count // step, body, 0)


def unrolled(count, body, step=4):
    def several(index, carry):
        for inner in range(step):
            body(index * step + inner)
        return carry

    lax.fori_loop(0, count // step, several, 0)


def place_kernel(groups, cap, cap_up, slot_ref, feat_ref, out_ref, rows, table):
    table[...] = jnp.zeros_like(table)

    def turn(i):
        block = feat_ref[i].astype(F32)
        rows[lane_block(i), :] = jnp.concatenate([block, block], axis=0).T

    unrolled(SAMPLES, turn)

    def move(s):
        table[pl.ds(slot_ref[s], 1), :] = rows[pl.ds(s, 1), :]

    move_rows(rows.shape[0], move)
    low = lax.broadcasted_iota(jnp.int32, (cap, LANES), 1) < ENC_WIDTH

    def pack(g, carry):
        first = table[pl.ds(pl.multiple_of(2 * g * cap_up, LANES), cap), :]
        second = table[pl.ds(pl.multiple_of((2 * g + 1) * cap_up, LANES), cap), :]
        out_ref[g] = jnp.where(low, first, second).astype(BF16)
        return carry

    lax.fori_loop(0, groups, pack, 0)


def greet(groups, me):
    barrier = pltpu.get_barrier_semaphore()

    def body(k, carry):
        pl.semaphore_signal(
            barrier, 1, device_id={"expert": lax.rem(me + k, groups)}, device_id_type=MESH
        )
        return carry

    lax.fori_loop(1, groups, body, 0)
    return barrier


def pad_first(wt_ref, m0):
    m0[...] = jnp.zeros_like(m0)
    for h in range(2):
        m0[h, ENC_WIDTH * h : ENC_WIDTH * (h + 1), :] = wt_ref[h, 0:ENC_WIDTH, :]


def layer_matrix(wt_ref, m0, h, layer):
    if layer == 0:
        return m0[h]
    start = ENC_WIDTH + (layer - 1) * NET_WIDTH
    return wt_ref[h, start : start + NET_WIDTH, :]


def tail_rows(wt_ref, h):
    return wt_ref[h, HEAD_ROW : HEAD_ROW + 16, :]


def forward(wt_ref, m0, block, keep=None):
    tails = [tail_rows(wt_ref, h).astype(F32) for h in range(2)]
    current = [block, block]
    for layer in range(LAYERS):
        for h in range(2):
            preact = dot(current[h], layer_matrix(wt_ref, m0, h, layer))
            preact = preact + tails[h][9 + layer : 10 + layer, :]
            current[h] = jnp.maximum(preact, 0.0).astype(BF16)
            if keep is not None:
                keep(layer, h, current[h])
    return current


def forward_kernel(
    groups, cap, cap_up, disp, params, arr, raw_out, wt, recv, msg, back, m0, tail_msg,
    master, master_sem, s1, r1, s2, r2,
):
    me = lax.axis_index("expert")
    load = pltpu.make_async_copy(params, master, master_sem)
    load.start()
    barrier = greet(groups, me)
    pl.semaphore_wait(barrier, groups - 1)

    def out_copy(k):
        peer = lax.rem(me + k, groups)
        return pltpu.make_async_remote_copy(
            disp.at[peer], recv.at[k], s1.at[k], r1.at[k],
            device_id={"expert": peer}, device_id_type=MESH,
        )

    def back_copy(k):
        peer = lax.rem(me + groups - k, groups)
        return pltpu.make_async_remote_copy(
            msg.at[k], back.at[me], s2.at[k], r2.at[k],
            device_id={"expert": peer}, device_id_type=MESH,
        )

    def start(k, carry):
        out_copy(k).start()
        return carry

    lax.fori_loop(1, groups, start, 0)
    load.wait()
    wt[...] = master[...].astype(BF16)
    pad_first(wt, m0)
    spot = lax.broadcasted_iota(jnp.int32, (4, LANES), 0) == lax.broadcasted_iota(
        jnp.int32, (4, LANES), 1
    )
    lane = lax.broadcasted_iota(jnp.int32, (4, LANES), 1)
    for h in range(2):
        tail = tail_rows(wt, h).astype(F32)
        column = jnp.sum(jnp.where(spot, tail[8:9, 0:LANES], 0.0), axis=1, keepdims=True)
        tail_msg[4 * h : 4 * h + 4, :] = jnp.where(
            lane < CODE_WIDTH, tail[4:8, 0:LANES], jnp.where(lane == CODE_WIDTH, column, 0.0)
        )

    def process(k, block):
        arr[k] = block
        msg[k, :, cap_up:] = tail_msg[...]
        if cap_up > cap:
            msg[k, :, cap:cap_up] = jnp.zeros((8, cap_up - cap), F32)
        acts = forward(wt, m0, block)
        for h in range(2):
            raw = dot(tail_rows(wt, h), acts[h], NT)
            msg[k, 4 * h : 4 * h + 4, 0:cap] = raw[0:4]

    process(0, disp[me])
    back[me] = msg[0]

    def step(k, carry):
        out_copy(k).wait_recv()
        process(k, recv[k])
        back_copy(k).start()
        return carry

    lax.fori_loop(1, groups, step, 0)

    def finish(k, carry):
        out_copy(k).wait_send()
        back_copy(k).wait_send()
        back_copy(k).wait_recv()
        return carry

    lax.fori_loop(1, groups, finish, 0)
    raw_out[...] = back[...]


def home_kernel(
    groups, cap_up, slot_ref, raw_ref, cell_ref, spacing_ref, length_ref, target_ref, image_ref,
    code_ref, first_ref, second_ref, loss_out, msg_out, code_out, first_out, second_out,
    rows, table, eight, mix, queries, shift,
):
    tiles = cap_up // LANES
    filler = jnp.zeros((LANES - 8, LANES), F32)

    def widen(g, carry):
        for t in range(tiles):
            piece = raw_ref[g, :, t * LANES : (t + 1) * LANES]
            turned = jnp.concatenate([piece, filler], axis=0).T
            for h in range(2):
                start = pl.multiple_of((2 * g + h) * cap_up + t * LANES, LANES)
                table[pl.ds(start, LANES), :] = turned
        block = pl.ds(pl.multiple_of(8 * g, 8), 8)
        queries[block, :] = raw_ref[g, :, cap_up : cap_up + CODE_WIDTH]
        shift[block, :] = jnp.broadcast_to(
            raw_ref[g, :, cap_up + CODE_WIDTH : cap_up + CODE_WIDTH + 1], (8, LANES)
        )
        return carry

    lax.fori_loop(0, groups, widen, 0)
    table[pl.ds(2 * groups * cap_up, 8), :] = jnp.zeros((8, LANES), F32)

    def take(s):
        rows[pl.ds(s, 1), :] = table[pl.ds(slot_ref[s], 1), :]

    move_rows(rows.shape[0], take)

    def narrow(i):
        eight[pl.ds(pl.multiple_of(8 * i, 8), 8), :] = rows[lane_block(i), :].T[0:8]

    unrolled(SAMPLES, narrow)
    table[...] = jnp.zeros_like(table)

    table_rows = code_ref.shape[0]
    pick = (
        lax.broadcasted_iota(jnp.int32, (table_rows, LANES), 0) == image_ref[...]
    ).astype(F32)
    code_bf = code_ref[...].astype(BF16).astype(F32)
    ray_code = exact(code_bf, pick, TN)
    mix[...] = exact(queries[...], ray_code) + shift[...]

    cell = cell_ref[...]
    odd = lax.rem(cell, 2) == 1
    row = lax.broadcasted_iota(jnp.int32, (SAMPLES, LANES), 0)
    live = row < length_ref[...]
    raws = tuple(
        jnp.where(
            odd, eight[pl.ds(4 + c, SAMPLES, 8), :], eight[pl.ds(c, SAMPLES, 8), :]
        )
        for c in range(4)
    )

    def add_code(g, raws):
        part = mix[pl.ds(pl.multiple_of(8 * g, 8), 8), :]
        raws = list(raws)
        for h in range(2):
            hit = cell == 2 * g + h
            for c in range(4):
                j = 4 * h + c
                raws[c] = raws[c] + jnp.where(hit, part[j : j + 1, :], 0.0)
        return tuple(raws)

    raws = lax.fori_loop(0, groups, add_code, raws)
    raws = [jnp.where(live, raw, 0.0) for raw in raws]
    spacing = spacing_ref[...]
    density = jnp.maximum(raws[0], 0.0) + jnp.log1p(jnp.exp(-jnp.abs(raws[0])))
    colors = [jax.nn.sigmoid(raw) for raw in raws[1:]]
    tau = jnp.where(live, density * spacing, 0.0)
    square_row = lax.broadcasted_iota(jnp.int32, (SAMPLES, SAMPLES), 0)
    square_col = lax.broadcasted_iota(jnp.int32, (SAMPLES, SAMPLES), 1)
    before = exact((square_col < square_row).astype(F32), tau)
    through = jnp.exp(-before)
    fade = jnp.exp(-tau)
    weight = through * (1.0 - fade)
    gaps = [
        jnp.sum(weight * colors[c], axis=0, keepdims=True) - target_ref[c : c + 1, :]
        for c in range(3)
    ]
    loss_out[...] = 0.5 * (gaps[0] * gaps[0] + gaps[1] * gaps[1] + gaps[2] * gaps[2])
    pull = gaps[0] * colors[0] + gaps[1] * colors[1] + gaps[2] * colors[2]
    after = exact((square_col > square_row).astype(F32), pull * weight)
    tau_grad = pull * through * fade - after
    grads = [tau_grad * spacing * jax.nn.sigmoid(raws[0])]
    for c in range(3):
        grads.append(gaps[c] * weight * colors[c] * (1.0 - colors[c]))
    cots = [jnp.where(live, grad, 0.0).astype(BF16).astype(F32) for grad in grads]
    for c in range(4):
        eight[pl.ds(c, SAMPLES, 8), :] = jnp.where(odd, 0.0, cots[c])
        eight[pl.ds(4 + c, SAMPLES, 8), :] = jnp.where(odd, cots[c], 0.0)

    def gather_code(g, carry):
        pieces = []
        for h in range(2):
            hit = cell == 2 * g + h
            for c in range(4):
                pieces.append(jnp.sum(jnp.where(hit, cots[c], 0.0), axis=0, keepdims=True))
        mix[pl.ds(pl.multiple_of(8 * g, 8), 8), :] = jnp.concatenate(pieces, axis=0)
        return carry

    lax.fori_loop(0, groups, gather_code, 0)
    totals = mix[...]
    query_grad = exact(totals, ray_code, NT)
    table_grad = exact(exact(totals, pick, NT), queries[...], TN)
    new_code, new_first, new_second = adam_update(
        code_ref[...], table_grad, first_ref[...], second_ref[...]
    )
    code_out[...] = new_code
    first_out[...] = new_first
    second_out[...] = new_second
    queries[...] = query_grad

    def widen_back(i):
        piece = eight[pl.ds(pl.multiple_of(8 * i, 8), 8), :]
        rows[lane_block(i), :] = jnp.concatenate([piece, filler], axis=0).T

    unrolled(SAMPLES, widen_back)

    def put(s):
        table[pl.ds(slot_ref[s], 1), :] = rows[pl.ds(s, 1), :]

    move_rows(rows.shape[0], put)

    def pack(g, carry):
        for t in range(tiles):
            start = [pl.multiple_of((2 * g + h) * cap_up + t * LANES, LANES) for h in range(2)]
            both = table[pl.ds(start[0], LANES), :] + table[pl.ds(start[1], LANES), :]
            msg_out[g, :, t * LANES : (t + 1) * LANES] = both.T[0:8]
        part = queries[pl.ds(pl.multiple_of(8 * g, 8), 8), :]
        msg_out[g, :, cap_up:] = jnp.concatenate(
            [part, jnp.zeros((8, LANES - CODE_WIDTH), F32)], axis=1
        )
        return carry

    lax.fori_loop(0, groups, pack, 0)


def backward_kernel(
    groups, cap, cap_up, msg, wt, arr, grad_out, recv, act, pre, m0, turned, head, code_sum,
    cot_sum, bias, grad, half_in, sum_out, sum_in, full, s1, r1, s2, r2,
):
    me = lax.axis_index("expert")
    my_dp = lax.axis_index("dp")
    core = lax.rem(my_dp, 2)
    near = my_dp + 1 - 2 * core
    far = my_dp + 2 - 4 * lax.rem(my_dp // 2, 2)
    barrier = greet(groups, me)
    for peer in (near, far):
        pl.semaphore_signal(barrier, 1, device_id={"dp": peer}, device_id_type=MESH)
    pl.semaphore_wait(barrier, groups + 1)

    def out_copy(k):
        peer = lax.rem(me + k, groups)
        return pltpu.make_async_remote_copy(
            msg.at[peer], recv.at[k], s1.at[k], r1.at[k],
            device_id={"expert": peer}, device_id_type=MESH,
        )

    def start(k, carry):
        out_copy(k).start()
        return carry

    lax.fori_loop(1, groups, start, 0)
    pad_first(wt, m0)
    head[...] = jnp.zeros_like(head)
    bias[...] = jnp.zeros_like(bias)
    for h in range(2):
        head[h, 4 * h : 4 * h + 4, :] = tail_rows(wt, h).astype(F32)[0:4]
        for layer in range(1, LAYERS):
            matrix = layer_matrix(wt, m0, h, layer)
            turned[layer - 1, h] = matrix.astype(F32).T.astype(BF16)

    pieces = 4
    size = arr.shape[0] // pieces

    def piece(index):
        return pl.ds(pl.multiple_of(index * size, 16), size)

    def again(index, carry):
        block = piece(index)

        def keep(layer, h, value):
            act[layer, h, block, :] = value

        forward(wt, m0, arr[block, :], keep)
        return carry

    lax.fori_loop(0, pieces, again, 0)
    recv[0] = msg[me]

    def arrive(k, carry):
        out_copy(k).wait()
        return carry

    lax.fori_loop(1, groups, arrive, 0)

    starts = [0] + [ENC_WIDTH + layer * NET_WIDTH for layer in range(LAYERS)] + [HEAD_ROW + 16]
    chunks = [pl.ds(starts[j], starts[j + 1] - starts[j]) for j in range(LAYERS + 1)]

    def near_copy(j):
        return pltpu.make_async_remote_copy(
            grad.at[1 - core, chunks[j]], half_in.at[chunks[j]],
            s2.at[0, j], r2.at[0, j], device_id={"dp": near}, device_id_type=MESH,
        )

    def far_copy(j):
        return pltpu.make_async_remote_copy(
            sum_out.at[chunks[j]], sum_in.at[chunks[j]],
            s2.at[1, j], r2.at[1, j], device_id={"dp": far}, device_id_type=MESH,
        )

    def full_copy(j, which):
        return pltpu.make_async_remote_copy(
            full.at[which, chunks[j]], full.at[which, chunks[j]],
            s2.at[2, j], r2.at[2, j], device_id={"dp": near}, device_id_type=MESH,
        )

    def second_stage(j):
        near_copy(j).wait_recv()
        rows = chunks[j]
        sum_out[rows, :] = (grad[core, rows, :] + half_in[rows, :]).astype(BF16)
        far_copy(j).start()

    def third_stage(j):
        far_copy(j).wait_recv()
        rows = chunks[j]
        full[core, rows, :] = sum_out[rows, :].astype(F32) + sum_in[rows, :].astype(F32)
        full_copy(j, core).start()

    top = LAYERS - 1
    heads_bf = [head[h].astype(BF16) for h in range(2)]

    def mask_store(layer, h, block, up):
        value = jnp.where(act[layer, h, block, :].astype(F32) > 0, up, 0.0).astype(BF16)
        pre[layer, h, block, :] = value
        bias[layer, h] += jnp.sum(
            value.astype(F32).reshape(-1, 8, NET_WIDTH), axis=0
        )

    code_sum[...] = jnp.zeros_like(code_sum)
    cot_sum[...] = jnp.zeros_like(cot_sum)

    def first_back(k, carry):
        block = pl.ds(pl.multiple_of(k * cap, 16), cap)
        cot = recv[k, :, 0:cap].astype(BF16)
        sums = []
        for h in range(2):
            mask_store(top, h, block, dot(cot, heads_bf[h], TN))
            sums.append(carry[h] + dot(cot, act[top, h, block, :]))
        code_sum[...] += recv[k, :, cap_up:]
        cot_sum[...] += jnp.broadcast_to(
            jnp.sum(recv[k, :, 0:cap], axis=1, keepdims=True), (8, LANES)
        )
        return tuple(sums)

    hidden = lax.fori_loop(
        0, groups, first_back, (jnp.zeros((8, NET_WIDTH), F32), jnp.zeros((8, NET_WIDTH), F32))
    )

    for layer in reversed(range(LAYERS)):
        if layer < top:

            def back(index, carry):
                block = piece(index)
                for h in range(2):
                    mask_store(
                        layer, h, block, dot(pre[layer + 1, h, block, :], turned[layer, h])
                    )
                return carry

            lax.fori_loop(0, pieces, back, 0)
        for h in range(2):
            if layer == 0:
                value = dot(arr[...], pre[0, h], TN)
                grad[h, 0:ENC_WIDTH, :] = value[ENC_WIDTH * h : ENC_WIDTH * (h + 1)]
            else:
                grad[h, chunks[layer], :] = dot(act[layer - 1, h], pre[layer, h], TN)
        near_copy(layer).start()
        if layer < top:
            second_stage(layer + 1)
        if layer < top - 1:
            third_stage(layer + 2)

    codes = jnp.concatenate([code_sum[...], jnp.zeros((8, NET_WIDTH - LANES), F32)], axis=1)
    spot = (
        lax.broadcasted_iota(jnp.int32, (8, LANES), 0)
        == lax.broadcasted_iota(jnp.int32, (8, LANES), 1)
    )
    cot_row = jnp.sum(jnp.where(spot, cot_sum[...], 0.0), axis=0, keepdims=True)
    lane = lax.broadcasted_iota(jnp.int32, (1, LANES), 1)
    for h in range(2):
        line = cot_row if h == 0 else pltpu.roll(cot_row, LANES - 4, 1)
        line = jnp.where(lane < 4, line, 0.0)
        line = jnp.concatenate([line, jnp.zeros((1, NET_WIDTH - LANES), F32)], axis=1)
        grad[h, HEAD_ROW : HEAD_ROW + 16, :] = jnp.concatenate(
            [hidden[h][4 * h : 4 * h + 4], codes[4 * h : 4 * h + 4], line]
            + [jnp.sum(bias[layer, h], axis=0, keepdims=True) for layer in range(LAYERS)]
            + [jnp.zeros((7 - LAYERS, NET_WIDTH), F32)],
            axis=0,
        )
    near_copy(LAYERS).start()
    second_stage(0)
    third_stage(1)
    second_stage(LAYERS)
    third_stage(0)
    third_stage(LAYERS)
    for j in (3, 2, 1, 0, LAYERS):
        near_copy(j).wait_send()
        far_copy(j).wait_send()
        full_copy(j, core).wait_send()
        full_copy(j, 1 - core).wait_recv()
        grad_out[:, chunks[j], :] = full[:, chunks[j], :]


def shards(
    features, spacing, targets, ray_length, cell_id, slot_rank, image_id,
    params, first_moment, second_moment, code_table, table_first, table_second,
):
    ray_rows = features.shape[0]
    sample_count = ray_rows * SAMPLES
    groups = lax.axis_size("expert")
    experts_all = params.shape[0] * groups
    cap = 2 * (sample_count * 3 // 4 // experts_all)
    cap_up = -(-cap // LANES) * LANES
    width = cap_up + LANES
    slots_up = experts_all * cap_up
    table_rows = code_table.shape[0]
    block_index = lax.axis_index("expert") * lax.axis_size("dp") + lax.axis_index("dp")
    local_image = (image_id - block_index * table_rows)[None, :]
    cell = cell_id.T
    rank = slot_rank.T
    slot = jnp.where(rank >= 0, cell * cap_up + rank, slots_up).reshape(sample_count)
    shape = jax.ShapeDtypeStruct
    big = 46 * 2**20
    table_scratch = pltpu.VMEM((slots_up + 8, LANES), F32)
    rows_scratch = pltpu.VMEM((sample_count, LANES), F32)
    msg_shape = (groups, 8, width)
    local = (sample_count + slots_up) * LANES * 4 + 8 * 2**20
    disp = pl.pallas_call(
        functools.partial(place_kernel, groups, cap, cap_up),
        out_shape=shape((groups, cap, LANES), BF16),
        in_specs=[SMEM, VMEM],
        out_specs=VMEM,
        scratch_shapes=[rows_scratch, table_scratch],
        compiler_params=pltpu.CompilerParams(vmem_limit_bytes=local),
        cost_estimate=pl.CostEstimate(flops=0, bytes_accessed=6000 * sample_count, transcendentals=0),
        name="place",
    )(slot, features.transpose(1, 2, 0))
    sems = pltpu.SemaphoreType.DMA((groups,))
    arr, raw_back, weights_bf = pl.pallas_call(
        functools.partial(forward_kernel, groups, cap, cap_up),
        out_shape=(
            shape((groups, cap, LANES), BF16), shape(msg_shape, F32), shape(params.shape, BF16),
        ),
        in_specs=[VMEM, pl.BlockSpec(memory_space=pltpu.HBM)],
        out_specs=(VMEM,) * 3,
        scratch_shapes=[
            pltpu.VMEM((groups, cap, LANES), BF16),
            pltpu.VMEM(msg_shape, F32),
            pltpu.VMEM(msg_shape, F32),
            pltpu.VMEM((2, LANES, NET_WIDTH), BF16),
            pltpu.VMEM((8, LANES), F32),
            pltpu.VMEM(params.shape, F32),
            pltpu.SemaphoreType.DMA,
            sems, sems, sems, sems,
        ],
        compiler_params=pltpu.CompilerParams(
            collective_id=0, has_side_effects=True, vmem_limit_bytes=32 * 2**20
        ),
        cost_estimate=pl.CostEstimate(flops=0, bytes_accessed=16000 * sample_count, transcendentals=0),
        name="dispatch",
    )(disp, params)
    table_shape = shape(code_table.shape, F32)
    loss, cot_msg, new_table, new_table_first, new_table_second = pl.pallas_call(
        functools.partial(home_kernel, groups, cap_up),
        out_shape=(
            shape((1, ray_rows), F32), shape(msg_shape, F32), table_shape, table_shape, table_shape,
        ),
        in_specs=[SMEM] + [VMEM] * 9,
        out_specs=(VMEM,) * 5,
        scratch_shapes=[
            rows_scratch,
            table_scratch,
            pltpu.VMEM((8 * SAMPLES, LANES), F32),
            pltpu.VMEM((8 * groups, LANES), F32),
            pltpu.VMEM((8 * groups, CODE_WIDTH), F32),
            pltpu.VMEM((8 * groups, LANES), F32),
        ],
        compiler_params=pltpu.CompilerParams(vmem_limit_bytes=local),
        cost_estimate=pl.CostEstimate(flops=0, bytes_accessed=12000 * sample_count, transcendentals=0),
        name="home",
    )(
        slot, raw_back, cell, spacing.T, ray_length[None, :], targets, local_image,
        code_table, table_first, table_second,
    )
    all_rows = groups * cap
    grad_rows = params.shape[1]
    param_grad = pl.pallas_call(
        functools.partial(backward_kernel, groups, cap, cap_up),
        out_shape=shape(params.shape, F32),
        in_specs=[VMEM] * 3,
        out_specs=VMEM,
        scratch_shapes=[
            pltpu.VMEM(msg_shape, F32),
            pltpu.VMEM((LAYERS, 2, all_rows, NET_WIDTH), BF16),
            pltpu.VMEM((LAYERS, 2, all_rows, NET_WIDTH), BF16),
            pltpu.VMEM((2, LANES, NET_WIDTH), BF16),
            pltpu.VMEM((LAYERS - 1, 2, NET_WIDTH, NET_WIDTH), BF16),
            pltpu.VMEM((2, 8, NET_WIDTH), F32),
            pltpu.VMEM((8, LANES), F32),
            pltpu.VMEM((8, LANES), F32),
            pltpu.VMEM((LAYERS, 2, 8, NET_WIDTH), F32),
            pltpu.VMEM((2, grad_rows, NET_WIDTH), F32),
            pltpu.VMEM((grad_rows, NET_WIDTH), F32),
            pltpu.VMEM((grad_rows, NET_WIDTH), BF16),
            pltpu.VMEM((grad_rows, NET_WIDTH), BF16),
            pltpu.VMEM((2, grad_rows, NET_WIDTH), F32),
            sems, sems,
            pltpu.SemaphoreType.DMA((3, LAYERS + 1)),
            pltpu.SemaphoreType.DMA((3, LAYERS + 1)),
        ],
        compiler_params=pltpu.CompilerParams(
            collective_id=1, has_side_effects=True, vmem_limit_bytes=big
        ),
        cost_estimate=pl.CostEstimate(flops=0, bytes_accessed=20000 * sample_count, transcendentals=0),
        name="backward",
    )(cot_msg, weights_bf, arr.reshape(all_rows, LANES))
    new_params, new_first, new_second = adam_update(params, param_grad, first_moment, second_moment)
    return (
        loss.reshape(ray_rows), new_params, new_first, new_second,
        new_table, new_table_first, new_table_second,
    )


def solution(mesh):
    both = ("expert", "dp")
    return jax.shard_map(
        shards,
        mesh=mesh,
        in_specs=(
            P(both, None, None), P(both, None), P(None, both), P(both), P(both, None),
            P(both, None), P(both),
            P("expert", None, None), P("expert", None, None), P("expert", None, None),
            P(both, None), P(both, None), P(both, None),
        ),
        out_specs=(
            P(both),
            P("expert", None, None), P("expert", None, None), P("expert", None, None),
            P(both, None), P(both, None), P(both, None),
        ),
        check_vma=False,
    )
```

profile of v0, /device:TPU:0, one launch (start us, length us, event | category | flops | bytes accessed | tf_op | source)
XLA Modules:
  0.0 89.7 jit_solution(9938297991563894870)
XLA Ops:
  0.6 0.7 subtract_bitcast_fusion.image_ref
  1.3 0.7 fusion.2.slot_ref
  2.0 0.0 copy-start.2
  2.0 1.0 %copy-done.2 = bf16[128,32,64]{0,2,1:T(8,128)(2,1)S(1)} copy-done((bf16[128,32,64]{0,2,1:T(8,128)(2,1)S(1)}, bf16[128,32,64]{0,2,1:T(8,128)(2,1)}, u32[]{:S(2)}) %copy-start.2) | copy-done | bytes 524312
  3.1 0.0 copy-start.7
  3.1 0.0 copy-start.8
  3.1 0.0 copy-start.9
  3.1 5.4 %place.1.disp = bf16[8,384,128]{2,1,0:T(8,128)(2,1)S(1)} custom-call(s32[4096]{0:T(1024)S(1)} %fusion.2.slot_ref, bf16[32,64,128]{2,1,0:T(8,128)(2,1)S(1)} %bitcast.21), custom_call_target="tpu_custom_call" | custom-call | bytes 24576000 | tf_op jit(solution)/shard_map/place/pallas_call | solution.py:555
  8.5 0.0 copy-start
  8.5 1.5 %copy-done = f32[2,848,256]{2,1,0:T(8,128)S(1)} copy-done((f32[2,848,256]{2,1,0:T(8,128)S(1)}, f32[2,848,256]{2,1,0:T(8,128)}, u32[]{:S(2)}) %copy-start) | copy-done | bytes 1736728
  10.0 33.9 %dispatch.1 = (bf16[8,384,128]{2,1,0:T(8,128)(2,1)S(1)}, f32[8,8,512]{2,1,0:T(8,128)S(1)}, bf16[2,848,256]{2,1,0:T(8,128)(2,1)S(1)}) custom-call(bf16[8,384,128]{2,1,0:T(8,128)(2,1)S(1)} %place.1.disp, f32[2,848,256]{2,1,0:T(8,128)S(1)} %copy-done), custom_call_target="tpu_custom_call" | custom-call | bytes 65536000 | tf_op jit(solution)/shard_map/dispatch/pallas_call | solution.py:566
  43.9 0.0 copy-done.3
  44.0 0.0 copy-done.4
  44.0 0.0 copy-done.5
  44.0 0.0 copy-done.6
  44.0 0.0 copy-done.7
  44.0 0.0 copy-done.8
  44.0 0.0 copy-done.9
  44.0 13.8 %home.1 = (f32[1,128]{1,0:T(1,128)}, f32[8,8,512]{2,1,0:T(8,128)S(1)}, f32[16,64]{1,0:T(8,128)}, f32[16,64]{1,0:T(8,128)}, f32[16,64]{1,0:T(8,128)}) custom-call(s32[4096]{0:T(1024)S(1)} %fusion.2.slot_ref, f32[8,8,512]{2,1,0:T(8,128)S(1)} %get-tuple-element.15.raw_ref, s32[32,128]{1,0:T(8,128)S(1)} %bitcast.22, f32[32,128]{1,0:T(8,128)S(1)} %bitcast.23, ...), custom_call_target="tpu_custom_call" | custom-call | bytes 49152000 | tf_op jit(solution)/shard_map/home/pallas_call | solution.py:590
  57.8 28.9 %backward.1 = f32[2,848,256]{2,1,0:T(8,128)S(1)} custom-call(f32[8,8,512]{2,1,0:T(8,128)S(1)} %get-tuple-element.17.msg, bf16[2,848,256]{2,1,0:T(8,128)(2,1)S(1)} %get-tuple-element.18.wt, bf16[3072,128]{1,0:T(8,128)(2,1)S(1)} %bitcast.20), custom_call_target="tpu_custom_call" | custom-call | bytes 81920000 | tf_op jit(solution)/shard_map/backward/pallas_call | solution.py:614
  86.7 0.0 copy-done.11
  86.7 0.0 copy-done.1
  86.7 0.0 copy-done.10
  86.7 3.0 %divide_subtract_fusion = (f32[2,848,256]{2,1,0:T(8,128)}, f32[2,848,256]{2,1,0:T(8,128)}, f32[2,848,256]{2,1,0:T(8,128)}) fusion(f32[2,848,256]{2,1,0:T(8,128)S(1)} %copy-done.1, f32[2,848,256]{2,1,0:T(8,128)S(1)} %backward.1, f32[2,848,256]{2,1,0:T(8,128)S(1)} %copy-done.10, f32[2,848,256]{2,1,0:T(8,128)S(1)} %copy-done.11), kind=kLoop, calls=%fused_computation.2 | loop fusion | flops 5210112 | bytes 12156928 | tf_op jit(solution)/shard_map/sub | solution.py:47
  (7 shorter events, 0.0 us)
Async XLA Ops:
  2.0 1.0 %copy-start.2 = (bf16[128,32,64]{0,2,1:T(8,128)(2,1)S(1)}, bf16[128,32,64]{0,2,1:T(8,128)(2,1)}, u32[]{:S(2)}) copy-start(bf16[128,32,64]{0,2,1:T(8,128)(2,1)} %param.13) | copy-start | bytes 1572868
  3.1 40.9 %copy-start.3 = (s32[128,32]{0,1:T(8,128)S(1)}, s32[128,32]{0,1:T(8,128)}, u32[]{:S(2)}) copy-start(s32[128,32]{0,1:T(8,128)} %param.17) | copy-start | bytes 49156
  3.1 40.9 %copy-start.4 = (f32[128,32]{0,1:T(8,128)S(1)}, f32[128,32]{0,1:T(8,128)}, u32[]{:S(2)}) copy-start(f32[128,32]{0,1:T(8,128)} %param.14) | copy-start | bytes 49156
  3.1 40.9 %copy-start.5 = (f32[16,64]{1,0:T(8,128)S(1)}, f32[16,64]{1,0:T(8,128)}, u32[]{:S(2)}) copy-start(f32[16,64]{1,0:T(8,128)} %code_ref.1) | copy-start | bytes 12292
  3.1 40.9 %copy-start.6 = (f32[16,64]{1,0:T(8,128)S(1)}, f32[16,64]{1,0:T(8,128)}, u32[]{:S(2)}) copy-start(f32[16,64]{1,0:T(8,128)} %first_ref.1) | copy-start | bytes 12292
  3.1 40.9 %copy-start.7 = (f32[16,64]{1,0:T(8,128)S(1)}, f32[16,64]{1,0:T(8,128)}, u32[]{:S(2)}) copy-start(f32[16,64]{1,0:T(8,128)} %second_ref.1) | copy-start | bytes 12292
  3.1 40.9 %copy-start.8 = (f32[3,128]{1,0:T(4,128)S(1)}, f32[3,128]{1,0:T(4,128)}, u32[]{:S(2)}) copy-start(f32[3,128]{1,0:T(4,128)} %target_ref.1) | copy-start | bytes 4612
  3.1 40.9 %copy-start.9 = (s32[128]{0:T(128)S(1)}, s32[128]{0:T(128)}, u32[]{:S(2)}) copy-start(s32[128]{0:T(128)} %param.16) | copy-start | bytes 1540
  8.5 1.5 %copy-start = (f32[2,848,256]{2,1,0:T(8,128)S(1)}, f32[2,848,256]{2,1,0:T(8,128)}, u32[]{:S(2)}) copy-start(f32[2,848,256]{2,1,0:T(8,128)} %params.1) | copy-start | bytes 5210116
  10.0 76.7 %copy-start.11 = (f32[2,848,256]{2,1,0:T(8,128)S(1)}, f32[2,848,256]{2,1,0:T(8,128)}, u32[]{:S(2)}) copy-start(f32[2,848,256]{2,1,0:T(8,128)} %param.22) | copy-start | bytes 5210116
  57.8 28.9 %copy-start.1 = (f32[2,848,256]{2,1,0:T(8,128)S(1)}, f32[2,848,256]{2,1,0:T(8,128)}, u32[]{:S(2)}) copy-start(f32[2,848,256]{2,1,0:T(8,128)} %params.1) | copy-start | bytes 5210116
  57.8 28.9 %copy-start.10 = (f32[2,848,256]{2,1,0:T(8,128)S(1)}, f32[2,848,256]{2,1,0:T(8,128)}, u32[]{:S(2)}) copy-start(f32[2,848,256]{2,1,0:T(8,128)} %param.21) | copy-start | bytes 5210116
where the time goes:
time: 90 us; the launch traced here: 89.7 us
  Pallas kernels  82 us (91%)
  other arithmetic  4.38 us (5%)
  local copies, waits for them, and re-layouts  2.55 us (3%)
    pallas_call x1, Pallas kernels, shards(): pl.pallas_call(functools.partial(forward_kernel, groups, cap, cap_up), ou...  33.9 us
    pallas_call x1, Pallas kernels, shards(): pl.pallas_call(functools.partial(backward_kernel, groups, cap, cap_up), o...  28.9 us
    pallas_call x1, Pallas kernels, shards(): pl.pallas_call(functools.partial(home_kernel, groups, cap_up), out_shape=...  13.8 us
    pallas_call x1, Pallas kernels, shards(): pl.pallas_call(functools.partial(place_kernel, groups, cap, cap_up), out_...  5.4 us
    sub x1, other arithmetic, adam_update(): return (param_now - update, new_one, new_two)  2.98 us
    unnamed x24, local copies, waits for them, and re-layouts  2.55 us

commit v1 on v0

v1 whole, which is shorter than its diff:
```python
import functools

import jax
import jax.numpy as jnp
from jax import lax
from jax.experimental import pallas as pl
from jax.experimental.pallas import tpu as pltpu
from jax.sharding import PartitionSpec as P

NET_WIDTH = 256
CODE_WIDTH = 64
ENC_WIDTH = 64
LAYERS = 4
SAMPLES = 32
HEAD_ROW = ENC_WIDTH + (LAYERS - 1) * NET_WIDTH
LANES = 128

BETA_ONE = 0.9
BETA_TWO = 0.999
LEARN_RATE = 0.001
ADAM_EPS = 1e-08
CORRECT_ONE = 1.0 - 0.9**10
CORRECT_TWO = 1.0 - 0.999**10

MESH = pl.DeviceIdType.MESH
VMEM = pl.BlockSpec(memory_space=pltpu.VMEM)
HBM = pl.BlockSpec(memory_space=pltpu.HBM)
F32 = jnp.float32
BF16 = jnp.bfloat16
NN = (((1,), (0,)), ((), ()))
NT = (((1,), (1,)), ((), ()))
TN = (((0,), (0,)), ((), ()))


def dot(left, right, dims=NN, precision=None):
    return lax.dot_general(left, right, dims, precision=precision, preferred_element_type=F32)


def exact(left, right, dims=NN):
    return dot(left, right, dims, lax.Precision.HIGHEST)


def adam_update(param_now, gradient, moment_one, moment_two):
    new_one = BETA_ONE * moment_one + (1.0 - BETA_ONE) * gradient
    new_two = BETA_TWO * moment_two + (1.0 - BETA_TWO) * gradient * gradient
    update = LEARN_RATE * (new_one / CORRECT_ONE) / (jnp.sqrt(new_two / CORRECT_TWO) + ADAM_EPS)
    return (param_now - update, new_one, new_two)


def iota(shape, dim):
    return lax.broadcasted_iota(jnp.int32, shape, dim)


def lane_block(index):
    return pl.ds(pl.multiple_of(index * LANES, LANES), LANES)


def rows_of(index, count, align=8):
    return pl.ds(pl.multiple_of(index * count, align), count)


def place_kernel(
    groups, cap, cap_up, cell_ref, rank_ref, feat_hbm, out_ref,
    feat, rows, table, counts, slot_vec, slot, feat_sem, slot_sem,
):
    load = pltpu.make_async_copy(feat_hbm, feat, feat_sem)
    load.start()
    cell = cell_ref[...]
    rank = rank_ref[...]
    live = rank >= 0
    slot_vec[...] = jnp.where(live, cell * cap_up + rank, 2 * groups * cap_up)
    scalars = pltpu.make_async_copy(slot_vec, slot, slot_sem)
    scalars.start()
    kind = jnp.where(live, cell, -1)

    def count(g, carry):
        parts = [
            jnp.sum(jnp.where(kind == 8 * g + j, 1.0, 0.0), axis=0, keepdims=True)
            for j in range(8)
        ]
        total = jnp.sum(jnp.concatenate(parts, axis=0), axis=1, keepdims=True)
        counts[rows_of(g, 8), :] = jnp.broadcast_to(total, (8, LANES))
        return carry

    lax.fori_loop(0, 2 * groups // 8, count, 0)
    load.wait()

    def turn(index, carry):
        for inner in range(4):
            i = index * 4 + inner
            block = feat[i].astype(F32)
            rows[lane_block(i), :] = jnp.concatenate([block, block], axis=0).T
        return carry

    lax.fori_loop(0, SAMPLES // 4, turn, 0)
    scalars.wait()
    for i in range(SAMPLES):

        def move(r, carry):
            table[pl.ds(slot[i, r], 1), :] = rows[pl.ds(i * LANES + r, 1), :]
            return carry

        lax.fori_loop(0, LANES, move, 0, unroll=True)
    low = iota((1, LANES), 1) < ENC_WIDTH
    position = iota((cap, LANES), 0).astype(F32)

    def pack(g, carry):
        first = table[pl.ds(pl.multiple_of(2 * g * cap_up, LANES), cap), :]
        second = table[pl.ds(pl.multiple_of((2 * g + 1) * cap_up, LANES), cap), :]
        limit = jnp.where(low, counts[pl.ds(2 * g, 1), :], counts[pl.ds(2 * g + 1, 1), :])
        value = jnp.where(low, first, second)
        out_ref[g] = jnp.where(position < limit, value, 0.0).astype(BF16)
        return carry

    lax.fori_loop(0, groups, pack, 0)


def flipped(me, k, groups):
    peer = 0
    bit = 1
    while bit < groups:
        peer = peer + bit * lax.rem(lax.div(me, bit) + lax.div(k, bit), 2)
        bit *= 2
    return peer


def layer_matrix(wt, m0, h, layer):
    if layer == 0:
        return m0[h]
    start = ENC_WIDTH + (layer - 1) * NET_WIDTH
    return wt[h, start : start + NET_WIDTH, :]


def tail_rows(wt, h):
    return wt[h, HEAD_ROW : HEAD_ROW + 16, :]


def prefix(value, row, backwards):
    step = 1
    while step < SAMPLES:
        if backwards:
            moved = jnp.where(row < SAMPLES - step, pltpu.roll(value, SAMPLES - step, 0), 0.0)
        else:
            moved = jnp.where(row >= step, pltpu.roll(value, step, 0), 0.0)
        value = value + moved
        step *= 2
    return value


def step_kernel(
    groups, cap, cap_up,
    disp, params, cell_ref, rank_ref, spacing_ref, length_ref, target_ref, image_ref,
    code_ref, first_ref, second_ref,
    grad_out, loss_out, code_out, first_out, second_out,
    master, tails_f32, wt, m0, turned, head, recv, act, pre,
    raw_msg, back, tail_msg, tails, queries, shift, mix, eight, keys, wide, spots,
    cot_msg, cot_in, code_msg, code_in, cot_sum, bias, grad, half_in, sum_out, sum_in, full,
    load_sems, s_out, r_out, s_back, r_back, s_tail, r_tail, s_cot, r_cot, s_code, r_code,
    s_sum, r_sum,
):
    tiles = cap_up // LANES
    half = max(groups // 2 - 1, 0)
    me = lax.axis_index("expert")
    my_dp = lax.axis_index("dp")
    core = lax.rem(my_dp, 2)
    near = my_dp + 1 - 2 * core
    far = my_dp + 2 - 4 * lax.rem(lax.div(my_dp, 2), 2)
    load_tail = pltpu.make_async_copy(
        params.at[:, HEAD_ROW : HEAD_ROW + 16, :], tails_f32, load_sems.at[0]
    )
    load_tail.start()
    load = pltpu.make_async_copy(params, master, load_sems.at[1])
    load.start()

    barrier = pltpu.get_barrier_semaphore()

    def greet(k, carry):
        pl.semaphore_signal(
            barrier, 1, device_id={"expert": lax.rem(me + k, groups)}, device_id_type=MESH
        )
        return carry

    lax.fori_loop(1, groups, greet, 0)
    for peer in (near, far):
        pl.semaphore_signal(barrier, 1, device_id={"dp": peer}, device_id_type=MESH)

    def turn_of(j):
        return lax.rem(j - 1 + half, groups - 1) + 1

    def block_rows(k):
        return rows_of(k, cap, 16)

    def peer_copy(k, source, target, sends, receives):
        return pltpu.make_async_remote_copy(
            source, target, sends.at[k], receives.at[k],
            device_id={"expert": flipped(me, k, groups)}, device_id_type=MESH,
        )

    def out_copy(k):
        return peer_copy(k, disp.at[flipped(me, k, groups)], recv.at[block_rows(k)], s_out, r_out)

    def back_copy(k):
        return peer_copy(k, raw_msg.at[k], back.at[me], s_back, r_back)

    def tail_copy(k):
        return peer_copy(k, tail_msg, tails.at[me], s_tail, r_tail)

    def cot_copy(k):
        return peer_copy(k, cot_msg.at[flipped(me, k, groups)], cot_in.at[k], s_cot, r_cot)

    def code_copy(k):
        return peer_copy(k, code_msg.at[flipped(me, k, groups)], code_in.at[k], s_code, r_code)

    def each(body):
        def turn(j, carry):
            body(turn_of(j))
            return carry

        lax.fori_loop(1, groups, turn, 0)

    load_tail.wait()
    spot = iota((4, LANES), 0) == iota((4, LANES), 1)
    lane = iota((4, LANES), 1)
    for h in range(2):
        tail = tails_f32[h].astype(BF16).astype(F32)
        column = jnp.sum(jnp.where(spot, tail[8:9, 0:LANES], 0.0), axis=1, keepdims=True)
        tail_msg[4 * h : 4 * h + 4, :] = jnp.where(
            lane < CODE_WIDTH, tail[4:8, 0:LANES], jnp.where(lane == CODE_WIDTH, column, 0.0)
        )
    tails[me] = tail_msg[...]
    pl.semaphore_wait(barrier, groups + 1)
    each(lambda k: tail_copy(k).start())
    each(lambda k: out_copy(k).start())

    load.wait()
    wt[...] = master[...].astype(BF16)
    m0[...] = jnp.zeros_like(m0)
    head[...] = jnp.zeros_like(head)
    for h in range(2):
        m0[h, ENC_WIDTH * h : ENC_WIDTH * (h + 1), :] = wt[h, 0:ENC_WIDTH, :]
        head[h, 4 * h : 4 * h + 4, :] = tail_rows(wt, h).astype(F32)[0:4]
    recv[block_rows(0), :] = disp[me]

    def process(k):
        block = block_rows(k)
        features = recv[block, :]
        biases = [tail_rows(wt, h).astype(F32) for h in range(2)]
        current = [features, features]
        for layer in range(LAYERS):
            for h in range(2):
                preact = dot(current[h], layer_matrix(wt, m0, h, layer))
                preact = preact + biases[h][9 + layer : 10 + layer, :]
                current[h] = jnp.maximum(preact, 0.0).astype(BF16)
                act[layer, h, block, :] = current[h]
        for h in range(2):
            raw = dot(tail_rows(wt, h), current[h], NT)
            raw_msg[k, 4 * h : 4 * h + 4, 0:cap] = raw[0:4]

    process(0)
    back[me] = raw_msg[0]

    for h in range(2):
        for layer in range(1, LAYERS):
            matrix = layer_matrix(wt, m0, h, layer)
            turned[layer - 1, h] = matrix.astype(F32).T.astype(BF16)

    cell = cell_ref[...]
    rank = rank_ref[...]
    row = iota((SAMPLES, LANES), 0)
    live = row < length_ref[...]
    place = jnp.where(live, rank, 0)
    tile = lax.div(place, LANES)
    lane_index = place - tile * LANES
    key = jnp.where(live, cell * tiles + tile, -1)
    table_rows = code_ref.shape[0]
    block_index = me * lax.axis_size("dp") + my_dp
    pick = (
        iota((table_rows, LANES), 0) == image_ref[...] - block_index * table_rows
    ).astype(F32)
    ray_code = exact(code_ref[...].astype(BF16).astype(F32), pick, TN)

    keys[...] = key.astype(F32)
    eight[0:SAMPLES, :] = lane_index.astype(F32)
    slot_lane = iota((LANES, LANES), 0).astype(F32)

    def spread(i, carry):
        line = jnp.broadcast_to(eight[pl.ds(i, 1), :], (LANES, LANES))
        spots[:, lane_block(i)] = jnp.where(line == slot_lane, 1.0, 0.0).astype(BF16)
        return carry

    lax.fori_loop(0, SAMPLES, spread, 0)

    def step(j, carry):
        k = turn_of(j)
        out_copy(k).wait_recv()
        process(k)
        back_copy(k).start()
        return carry

    lax.fori_loop(1, groups, step, 0)

    each(lambda k: tail_copy(k).wait_recv())

    def collect(g, carry):
        queries[rows_of(g, 8), :] = tails[g, :, 0:CODE_WIDTH]
        shift[rows_of(g, 8), :] = jnp.broadcast_to(
            tails[g, :, CODE_WIDTH : CODE_WIDTH + 1], (8, LANES)
        )
        return carry

    lax.fori_loop(0, groups, collect, 0)
    mix[...] = exact(queries[...], ray_code) + shift[...]
    zero = jnp.zeros((SAMPLES, LANES), F32)

    def add_code(g, codes):
        part = mix[rows_of(g, 8), :]
        codes = list(codes)
        for h in range(2):
            hit = cell == 2 * g + h
            for c in range(4):
                j = 4 * h + c
                codes[c] = jnp.where(hit, part[j : j + 1, :], codes[c])
        return tuple(codes)

    codes = lax.fori_loop(0, groups, add_code, (zero,) * 4)

    def take(g, raws):
        raws = list(raws)
        for t in range(tiles):
            piece = back[g, :, t * LANES : (t + 1) * LANES]
            for h in range(2):
                hit = key == (2 * g + h) * tiles + t
                for c in range(4):
                    j = 4 * h + c
                    line = jnp.broadcast_to(piece[j : j + 1, :], (SAMPLES, LANES))
                    found = jnp.take_along_axis(line, lane_index, axis=1)
                    raws[c] = jnp.where(hit, found, raws[c])
        return tuple(raws)

    raws = take(me, (zero,) * 4)

    def take_next(j, raws):
        k = turn_of(j)
        back_copy(k).wait_recv()
        return take(flipped(me, k, groups), raws)

    raws = lax.fori_loop(1, groups, take_next, raws)
    raws = [jnp.where(live, raws[c] + codes[c], 0.0) for c in range(4)]
    spacing = spacing_ref[...]
    density = jnp.maximum(raws[0], 0.0) + jnp.log1p(jnp.exp(-jnp.abs(raws[0])))
    colors = [jax.nn.sigmoid(raw) for raw in raws[1:]]
    tau = jnp.where(live, density * spacing, 0.0)
    before = prefix(tau, row, False) - tau
    through = jnp.exp(-before)
    fade = jnp.exp(-tau)
    weight = through * (1.0 - fade)
    gaps = [
        jnp.sum(weight * colors[c], axis=0, keepdims=True) - target_ref[c : c + 1, :]
        for c in range(3)
    ]
    loss_out[...] = 0.5 * (gaps[0] * gaps[0] + gaps[1] * gaps[1] + gaps[2] * gaps[2])
    pull = gaps[0] * colors[0] + gaps[1] * colors[1] + gaps[2] * colors[2]
    gain = pull * weight
    after = prefix(gain, row, True) - gain
    tau_grad = pull * through * fade - after
    grads = [tau_grad * spacing * jax.nn.sigmoid(raws[0])]
    for c in range(3):
        grads.append(gaps[c] * weight * colors[c] * (1.0 - colors[c]))
    for c in range(4):
        cot = jnp.where(live, grads[c], 0.0).astype(BF16).astype(F32)
        eight[pl.ds(c, SAMPLES, 8), :] = cot
        eight[pl.ds(4 + c, SAMPLES, 8), :] = cot
    mix[...] = jnp.zeros_like(mix)
    member = lax.div(iota((8, LANES), 0), 4) * tiles

    def widen(i, carry):
        value = eight[rows_of(i, 8), :]
        line = jnp.broadcast_to(keys[pl.ds(i, 1), :], (8, LANES))
        sums = [0.0] * groups
        for t in range(tiles):
            for pair in range(groups // 2):
                both = []
                for g in (2 * pair, 2 * pair + 1):
                    want = (member + (2 * g * tiles + t)).astype(F32)
                    chosen = jnp.where(line == want, value, 0.0)
                    sums[g] = sums[g] + chosen
                    both.append(chosen)
                start = (t * groups + 2 * pair) * 8
                wide[start : start + 16, lane_block(i)] = jnp.concatenate(both, axis=0).astype(BF16)
        for g in range(groups):
            mix[8 * g : 8 * g + 8, :] += sums[g]
        return carry

    lax.fori_loop(0, SAMPLES, widen, 0)
    slots = dot(wide[...], spots[...], NT)
    for t in range(tiles):
        for g in range(groups):
            start = (t * groups + g) * 8
            cot_msg[g, :, t * LANES : (t + 1) * LANES] = slots[start : start + 8].astype(BF16)
    each(lambda k: cot_copy(k).start())
    cot_in[0] = cot_msg[me]

    totals = mix[...]
    query_grad = exact(totals, ray_code, NT)
    for g in range(groups):
        code_msg[g, :, 0:CODE_WIDTH] = query_grad[8 * g : 8 * g + 8]
        code_msg[g, :, CODE_WIDTH:] = jnp.zeros((8, LANES - CODE_WIDTH), F32)
    each(lambda k: code_copy(k).start())
    code_in[0] = code_msg[me]
    table_grad = exact(exact(totals, pick, NT), queries[...], TN)
    new_code, new_first, new_second = adam_update(
        code_ref[...], table_grad, first_ref[...], second_ref[...]
    )
    code_out[...] = new_code
    first_out[...] = new_first
    second_out[...] = new_second

    starts = [0] + [ENC_WIDTH + layer * NET_WIDTH for layer in range(LAYERS)] + [HEAD_ROW + 16]
    chunks = [pl.ds(starts[j], starts[j + 1] - starts[j]) for j in range(LAYERS + 1)]

    def near_copy(j):
        return pltpu.make_async_remote_copy(
            grad.at[1 - core, chunks[j]], half_in.at[chunks[j]],
            s_sum.at[0, j], r_sum.at[0, j], device_id={"dp": near}, device_id_type=MESH,
        )

    def far_copy(j):
        return pltpu.make_async_remote_copy(
            sum_out.at[chunks[j]], sum_in.at[chunks[j]],
            s_sum.at[1, j], r_sum.at[1, j], device_id={"dp": far}, device_id_type=MESH,
        )

    def full_copy(j, which):
        return pltpu.make_async_remote_copy(
            full.at[which, chunks[j]], full.at[which, chunks[j]],
            s_sum.at[2, j], r_sum.at[2, j], device_id={"dp": near}, device_id_type=MESH,
        )

    def second_stage(j):
        near_copy(j).wait_recv()
        rows = chunks[j]
        sum_out[rows, :] = (grad[core, rows, :] + half_in[rows, :]).astype(BF16)
        far_copy(j).start()

    def third_stage(j):
        far_copy(j).wait_recv()
        rows = chunks[j]
        full[core, rows, :] = sum_out[rows, :].astype(F32) + sum_in[rows, :].astype(F32)
        full_copy(j, core).start()

    top = LAYERS - 1
    heads_bf = [head[h].astype(BF16) for h in range(2)]
    bias[...] = jnp.zeros_like(bias)
    cot_sum[...] = jnp.zeros_like(cot_sum)

    def mask_store(layer, h, block, up):
        value = jnp.where(act[layer, h, block, :].astype(F32) > 0, up, 0.0).astype(BF16)
        pre[layer, h, block, :] = value
        bias[layer, h] += jnp.sum(value.astype(F32).reshape(-1, 8, NET_WIDTH), axis=0)

    def first_back(k, carry):
        block = block_rows(k)
        cot = cot_in[k, :, 0:cap]
        sums = []
        for h in range(2):
            mask_store(top, h, block, dot(cot, heads_bf[h], TN))
            sums.append(carry[h] + dot(cot, act[top, h, block, :]))
        cot_sum[...] += jnp.broadcast_to(
            jnp.sum(cot.astype(F32), axis=1, keepdims=True), (8, LANES)
        )
        return tuple(sums)

    def next_back(j, carry):
        k = turn_of(j)
        cot_copy(k).wait_recv()
        return first_back(k, carry)

    zeros = jnp.zeros((8, NET_WIDTH), F32)
    hidden = lax.fori_loop(1, groups, next_back, first_back(0, (zeros, zeros)))

    pieces = 4
    size = recv.shape[0] // pieces
    for layer in reversed(range(LAYERS)):
        if layer < top:

            def onward(index, carry):
                block = rows_of(index, size, 16)
                for h in range(2):
                    mask_store(
                        layer, h, block, dot(pre[layer + 1, h, block, :], turned[layer, h])
                    )
                return carry

            lax.fori_loop(0, pieces, onward, 0)
        for h in range(2):
            if layer == 0:
                value = dot(recv[...], pre[0, h], TN)
                grad[h, 0:ENC_WIDTH, :] = value[ENC_WIDTH * h : ENC_WIDTH * (h + 1)]
            else:
                grad[h, chunks[layer], :] = dot(act[layer - 1, h], pre[layer, h], TN)
        near_copy(layer).start()
        if layer < top:
            second_stage(layer + 1)
        if layer < top - 1:
            third_stage(layer + 2)

    def add_codes(k, carry):
        code_copy(k).wait_recv()
        return carry + code_in[k]

    code_sum = lax.fori_loop(1, groups, add_codes, code_in[0])
    codes = jnp.concatenate([code_sum, jnp.zeros((8, NET_WIDTH - LANES), F32)], axis=1)
    spot = iota((8, LANES), 0) == iota((8, LANES), 1)
    cot_row = jnp.sum(jnp.where(spot, cot_sum[...], 0.0), axis=0, keepdims=True)
    lane = iota((1, LANES), 1)
    for h in range(2):
        line = cot_row if h == 0 else pltpu.roll(cot_row, LANES - 4, 1)
        line = jnp.where(lane < 4, line, 0.0)
        line = jnp.concatenate([line, jnp.zeros((1, NET_WIDTH - LANES), F32)], axis=1)
        grad[h, HEAD_ROW : HEAD_ROW + 16, :] = jnp.concatenate(
            [hidden[h][4 * h : 4 * h + 4], codes[4 * h : 4 * h + 4], line]
            + [jnp.sum(bias[layer, h], axis=0, keepdims=True) for layer in range(LAYERS)]
            + [jnp.zeros((7 - LAYERS, NET_WIDTH), F32)],
            axis=0,
        )
    near_copy(LAYERS).start()
    second_stage(0)
    third_stage(1)
    second_stage(LAYERS)
    third_stage(0)
    third_stage(LAYERS)

    def drain(k):
        for copy in (tail_copy, out_copy, back_copy, cot_copy, code_copy):
            copy(k).wait_send()

    each(drain)
    for j in (3, 2, 1, 0, LAYERS):
        near_copy(j).wait_send()
        far_copy(j).wait_send()
        full_copy(j, core).wait_send()
        full_copy(j, 1 - core).wait_recv()
        grad_out[:, chunks[j], :] = full[:, chunks[j], :]


def shards(
    features, spacing, targets, ray_length, cell_id, slot_rank, image_id,
    params, first_moment, second_moment, code_table, table_first, table_second,
):
    ray_rows = features.shape[0]
    sample_count = ray_rows * SAMPLES
    groups = lax.axis_size("expert")
    experts_all = params.shape[0] * groups
    cap = 2 * (sample_count * 3 // 4 // experts_all)
    cap_up = -(-cap // LANES) * LANES
    tiles = cap_up // LANES
    slots_up = experts_all * cap_up
    shape = jax.ShapeDtypeStruct
    scratch = pltpu.VMEM
    sem = pltpu.SemaphoreType.DMA
    cell = cell_id.T
    rank = slot_rank.T
    disp = pl.pallas_call(
        functools.partial(place_kernel, groups, cap, cap_up),
        out_shape=shape((groups, cap, LANES), BF16),
        in_specs=[VMEM, VMEM, HBM],
        out_specs=VMEM,
        scratch_shapes=[
            scratch((SAMPLES, ENC_WIDTH, ray_rows), BF16),
            scratch((sample_count, LANES), F32),
            scratch((slots_up + 8, LANES), F32),
            scratch((experts_all, LANES), F32),
            scratch((SAMPLES, LANES), jnp.int32),
            pltpu.SMEM((SAMPLES, LANES), jnp.int32),
            sem, sem,
        ],
        compiler_params=pltpu.CompilerParams(vmem_limit_bytes=48 * 2**20),
        cost_estimate=pl.CostEstimate(flops=0, bytes_accessed=6000 * sample_count, transcendentals=0),
        name="place",
    )(cell, rank, features.transpose(1, 2, 0))
    all_rows = groups * cap
    grad_rows = params.shape[1]
    table_shape = shape(code_table.shape, F32)
    peers = sem((groups,))
    param_grad, loss, new_table, new_table_first, new_table_second = pl.pallas_call(
        functools.partial(step_kernel, groups, cap, cap_up),
        out_shape=(
            shape(params.shape, F32), shape((1, ray_rows), F32), table_shape, table_shape, table_shape,
        ),
        in_specs=[VMEM, HBM] + [VMEM] * 9,
        out_specs=(VMEM,) * 5,
        scratch_shapes=[
            scratch(params.shape, F32),
            scratch((2, 16, NET_WIDTH), F32),
            scratch(params.shape, BF16),
            scratch((2, LANES, NET_WIDTH), BF16),
            scratch((LAYERS - 1, 2, NET_WIDTH, NET_WIDTH), BF16),
            scratch((2, 8, NET_WIDTH), F32),
            scratch((all_rows, LANES), BF16),
            scratch((LAYERS, 2, all_rows, NET_WIDTH), BF16),
            scratch((LAYERS, 2, all_rows, NET_WIDTH), BF16),
            scratch((groups, 8, cap_up), F32),
            scratch((groups, 8, cap_up), F32),
            scratch((8, LANES), F32),
            scratch((groups, 8, LANES), F32),
            scratch((8 * groups, CODE_WIDTH), F32),
            scratch((8 * groups, LANES), F32),
            scratch((8 * groups, LANES), F32),
            scratch((8 * SAMPLES, LANES), F32),
            scratch((SAMPLES, LANES), F32),
            scratch((tiles * groups * 8, sample_count), BF16),
            scratch((LANES, sample_count), BF16),
            scratch((groups, 8, cap_up), BF16),
            scratch((groups, 8, cap_up), BF16),
            scratch((groups, 8, LANES), F32),
            scratch((groups, 8, LANES), F32),
            scratch((8, LANES), F32),
            scratch((LAYERS, 2, 8, NET_WIDTH), F32),
            scratch((2, grad_rows, NET_WIDTH), F32),
            scratch((grad_rows, NET_WIDTH), F32),
            scratch((grad_rows, NET_WIDTH), BF16),
            scratch((grad_rows, NET_WIDTH), BF16),
            scratch((2, grad_rows, NET_WIDTH), F32),
            sem((2,)),
            peers, peers, peers, peers, peers, peers, peers, peers, peers, peers,
            sem((3, LAYERS + 1)),
            sem((3, LAYERS + 1)),
        ],
        compiler_params=pltpu.CompilerParams(
            collective_id=0, has_side_effects=True, vmem_limit_bytes=52 * 2**20
        ),
        cost_estimate=pl.CostEstimate(flops=0, bytes_accessed=50000 * sample_count, transcendentals=0),
        name="step",
    )(
        disp, params, cell, rank, spacing.T, ray_length[None, :], targets, image_id[None, :],
        code_table, table_first, table_second,
    )
    new_params, new_first, new_second = adam_update(params, param_grad, first_moment, second_moment)
    return (
        loss.reshape(ray_rows), new_params, new_first, new_second,
        new_table, new_table_first, new_table_second,
    )


def solution(mesh):
    both = ("expert", "dp")
    return jax.shard_map(
        shards,
        mesh=mesh,
        in_specs=(
            P(both, None, None), P(both, None), P(None, both), P(both), P(both, None),
            P(both, None), P(both),
            P("expert", None, None), P("expert", None, None), P("expert", None, None),
            P(both, None), P(both, None), P(both, None),
        ),
        out_specs=(
            P(both),
            P("expert", None, None), P("expert", None, None), P("expert", None, None),
            P(both, None), P(both, None), P(both, None),
        ),
        check_vma=False,
    )
```

time: 90 us -> 83 us (0.922)
  Pallas kernels: 82 us -> 65 us
  local copies, waits for them, and re-layouts: 2.55 us -> 11 us
  other arithmetic: 4.38 us -> 5.48 us
    pallas_call x3 -> x1, Pallas kernels: 76.6 us -> 61.6 us  [shards(): pl.pallas_call(functools.partial(step_kernel, groups, cap, cap_up), out_s...]
    unnamed x24 -> x30, local copies, waits for them, and re-layouts: 2.55 us -> 11 us
    sub x1, other arithmetic: 2.98 us -> 5.48 us  [adam_update(): return (param_now - update, new_one, new_two)]
    pallas_call x1, Pallas kernels: 5.4 us -> 3.49 us  [shards(): pl.pallas_call(functools.partial(place_kernel, groups, cap, cap_up), out_...]
where the time goes in v1:
time: 83 us; the launch traced here: 82.2 us
  Pallas kernels  65 us (78%)
  local copies, waits for them, and re-layouts  11 us (13%)
  other arithmetic  5.48 us (7%)
    pallas_call x1, Pallas kernels, shards(): pl.pallas_call(functools.partial(step_kernel, groups, cap, cap_up), out_s...  61.6 us
    unnamed x30, local copies, waits for them, and re-layouts  11 us
    sub x1, other arithmetic, adam_update(): return (param_now - update, new_one, new_two)  5.48 us
    pallas_call x1, Pallas kernels, shards(): pl.pallas_call(functools.partial(place_kernel, groups, cap, cap_up), out_...  3.49 us

profile of v1, /device:TPU:0, one launch (start us, length us, event | category | flops | bytes accessed | tf_op | source)
XLA Modules:
  0.0 82.2 jit_solution(2384836105031648794)
XLA Ops:
  0.6 0.0 copy-start
  0.6 1.0 %copy-done = bf16[128,32,64]{0,2,1:T(8,128)(2,1)S(1)} copy-done((bf16[128,32,64]{0,2,1:T(8,128)(2,1)S(1)}, bf16[128,32,64]{0,2,1:T(8,128)(2,1)}, u32[]{:S(2)}) %copy-start) | copy-done | bytes 524312
  1.7 0.0 copy-start.1
  1.7 0.7 copy-done.1
  2.4 0.0 copy-start.3
  2.4 0.7 copy-done.3
  3.1 3.5 %place.1.disp = bf16[8,384,128]{2,1,0:T(8,128)(2,1)S(1)} custom-call(s32[32,128]{1,0:T(8,128)S(1)} %bitcast.8, s32[32,128]{1,0:T(8,128)S(1)} %bitcast.10, bf16[32,64,128]{2,1,0:T(8,128)(2,1)S(1)} %bitcast.7), custom_call_target="tpu_custom_call" | custom-call | bytes 24576000 | tf_op jit(solution)/shard_map/place/pallas_call | solution.py:563
  6.6 0.0 copy-start.2
  6.6 0.7 copy-done.2
  7.3 0.7 copy-done.4
  8.0 0.7 copy-done.5
  8.8 0.7 copy-done.6
  9.5 0.7 copy-done.7
  10.2 0.7 copy-done.8
  10.9 0.7 copy-done.9
  11.5 0.7 copy-done.10
  12.2 0.7 copy-done.11
  12.8 61.6 %step.1 = (f32[2,848,256]{2,1,0:T(8,128)}, f32[1,128]{1,0:T(1,128)S(1)}, f32[16,64]{1,0:T(8,128)S(1)}, f32[16,64]{1,0:T(8,128)S(1)}, f32[16,64]{1,0:T(8,128)S(1)}) custom-call(bf16[8,384,128]{2,1,0:T(8,128)(2,1)S(1)} %place.1.disp, f32[2,848,256]{2,1,0:T(8,128)} %params.1, s32[32,128]{1,0:T(8,128)S(1)} %bitcast.9, s32[32,128]{1,0:T(8,128)S(1)} %bitcast.11, ...), custom_call_target="tpu_custom_call" | custom-call | bytes 204800000 | tf_op jit(solution)/shard_map/step/pallas_call | solution.py:585
  74.4 0.0 copy-done.12
  74.4 5.5 %divide_subtract_fusion = (f32[2,848,256]{2,1,0:T(8,128)}, f32[2,848,256]{2,1,0:T(8,128)}, f32[2,848,256]{2,1,0:T(8,128)}) fusion(f32[2,848,256]{2,1,0:T(8,128)S(1)} %copy-done.12, f32[2,848,256]{2,1,0:T(8,128)} %get-tuple-element.13, f32[2,848,256]{2,1,0:T(8,128)} %param.21, f32[2,848,256]{2,1,0:T(8,128)} %param.22), kind=kLoop, calls=%fused_computation.2 | loop fusion | flops 5210112 | bytes 12156928 | tf_op jit(solution)/shard_map/sub | solution.py:47
  79.9 0.5 copy.24
  80.4 0.6 copy.25
  81.0 0.6 copy.26
  81.6 0.6 copy.27
  (9 shorter events, 0.0 us)
Async XLA Ops:
  0.6 1.0 %copy-start = (bf16[128,32,64]{0,2,1:T(8,128)(2,1)S(1)}, bf16[128,32,64]{0,2,1:T(8,128)(2,1)}, u32[]{:S(2)}) copy-start(bf16[128,32,64]{0,2,1:T(8,128)(2,1)} %param.13) | copy-start | bytes 1572868
  1.7 0.7 copy-start.1
  2.4 0.7 copy-start.3
  6.6 0.7 copy-start.2
  7.3 0.7 copy-start.4
  8.0 0.7 copy-start.5
  8.8 0.7 copy-start.6
  9.5 0.7 copy-start.7
  10.2 0.7 copy-start.8
  10.9 0.7 copy-start.9
  11.5 0.7 copy-start.10
  12.2 0.7 copy-start.11
  12.8 61.6 %copy-start.12 = (f32[2,848,256]{2,1,0:T(8,128)S(1)}, f32[2,848,256]{2,1,0:T(8,128)}, u32[]{:S(2)}) copy-start(f32[2,848,256]{2,1,0:T(8,128)} %params.1) | copy-start | bytes 5210116

commit v2 on v1

--- a/solution.py
+++ b/solution.py
@@ -60,11 +60,22 @@
 
 
 def place_kernel(
-    groups, cap, cap_up, cell_ref, rank_ref, feat_hbm, out_ref,
-    feat, rows, table, counts, slot_vec, slot, feat_sem, slot_sem,
+    groups, cap, cap_up, cell_hbm, rank_hbm, feat_hbm, params_hbm, *refs,
 ):
-    load = pltpu.make_async_copy(feat_hbm, feat, feat_sem)
-    load.start()
+    smalls = refs[:7]
+    out_ref, wt, cell_ref, rank_ref = refs[7:11]
+    small_outs = refs[11:18]
+    master, feat, rows, table, counts, slot_vec, slot, load_sems, slot_sem = refs[18:]
+    pairs = [(cell_hbm, cell_ref), (rank_hbm, rank_ref), (feat_hbm, feat), (params_hbm, master)]
+    pairs += list(zip(smalls, small_outs))
+    loads = [
+        pltpu.make_async_copy(source, target, load_sems.at[n])
+        for n, (source, target) in enumerate(pairs)
+    ]
+    for load in loads:
+        load.start()
+    loads[0].wait()
+    loads[1].wait()
     cell = cell_ref[...]
     rank = rank_ref[...]
     live = rank >= 0
@@ -83,7 +94,7 @@
         return carry
 
     lax.fori_loop(0, 2 * groups // 8, count, 0)
-    load.wait()
+    loads[2].wait()
 
     def turn(index, carry):
         for inner in range(4):
@@ -113,6 +124,9 @@
         return carry
 
     lax.fori_loop(0, groups, pack, 0)
+    for load in loads[3:]:
+        load.wait()
+    wt[...] = master[...].astype(BF16)
 
 
 def flipped(me, k, groups):
@@ -149,13 +163,13 @@
 
 def step_kernel(
     groups, cap, cap_up,
-    disp, params, cell_ref, rank_ref, spacing_ref, length_ref, target_ref, image_ref,
+    disp, wt, cell_ref, rank_ref, spacing_ref, length_ref, target_ref, image_ref,
     code_ref, first_ref, second_ref,
     grad_out, loss_out, code_out, first_out, second_out,
-    master, tails_f32, wt, m0, turned, head, recv, act, pre,
+    m0, turned, head, recv, act, pre,
     raw_msg, back, tail_msg, tails, queries, shift, mix, eight, keys, wide, spots,
     cot_msg, cot_in, code_msg, code_in, cot_sum, bias, grad, half_in, sum_out, sum_in, full,
-    load_sems, s_out, r_out, s_back, r_back, s_tail, r_tail, s_cot, r_cot, s_code, r_code,
+    s_out, r_out, s_back, r_back, s_tail, r_tail, s_cot, r_cot, s_code, r_code,
     s_sum, r_sum,
 ):
     tiles = cap_up // LANES
@@ -165,13 +179,6 @@
     core = lax.rem(my_dp, 2)
     near = my_dp + 1 - 2 * core
     far = my_dp + 2 - 4 * lax.rem(lax.div(my_dp, 2), 2)
-    load_tail = pltpu.make_async_copy(
-        params.at[:, HEAD_ROW : HEAD_ROW + 16, :], tails_f32, load_sems.at[0]
-    )
-    load_tail.start()
-    load = pltpu.make_async_copy(params, master, load_sems.at[1])
-    load.start()
-
     barrier = pltpu.get_barrier_semaphore()
 
     def greet(k, carry):
@@ -218,11 +225,10 @@
 
         lax.fori_loop(1, groups, turn, 0)
 
-    load_tail.wait()
     spot = iota((4, LANES), 0) == iota((4, LANES), 1)
     lane = iota((4, LANES), 1)
     for h in range(2):
-        tail = tails_f32[h].astype(BF16).astype(F32)
+        tail = tail_rows(wt, h).astype(F32)
         column = jnp.sum(jnp.where(spot, tail[8:9, 0:LANES], 0.0), axis=1, keepdims=True)
         tail_msg[4 * h : 4 * h + 4, :] = jnp.where(
             lane < CODE_WIDTH, tail[4:8, 0:LANES], jnp.where(lane == CODE_WIDTH, column, 0.0)
@@ -232,8 +238,6 @@
     each(lambda k: tail_copy(k).start())
     each(lambda k: out_copy(k).start())
 
-    load.wait()
-    wt[...] = master[...].astype(BF16)
     m0[...] = jnp.zeros_like(m0)
     head[...] = jnp.zeros_like(head)
     for h in range(2):
@@ -543,6 +547,32 @@
         grad_out[:, chunks[j], :] = full[:, chunks[j], :]
 
 
+def update_kernel(*refs):
+    grad, params, first, second = refs[:4]
+    smalls, large_outs, small_outs = refs[4:8], refs[8:11], refs[11:15]
+    stages, large_sems, small_sems = refs[15:18], refs[18], refs[19]
+    copies = [
+        pltpu.make_async_copy(source, target, small_sems.at[n])
+        for n, (source, target) in enumerate(zip(smalls, small_outs))
+    ]
+    for copy in copies:
+        copy.start()
+    half = grad.shape[1] // 2
+    for part in range(4):
+        rows = pl.ds(part % 2 * half, half)
+        spot = (part // 2, rows, slice(None))
+        values = adam_update(params[spot], grad[spot], first[spot], second[spot])
+        for n in range(3):
+            stages[n][spot] = values[n]
+            copy = pltpu.make_async_copy(
+                stages[n].at[spot], large_outs[n].at[spot], large_sems.at[n, part]
+            )
+            copy.start()
+            copies.append(copy)
+    for copy in copies:
+        copy.wait()
+
+
 def shards(
     features, spacing, targets, ray_length, cell_id, slot_rank, image_id,
     params, first_moment, second_moment, code_table, table_first, table_second,
@@ -554,17 +584,26 @@
     cap = 2 * (sample_count * 3 // 4 // experts_all)
     cap_up = -(-cap // LANES) * LANES
     tiles = cap_up // LANES
+    wide_rows = tiles * groups * 8
     slots_up = experts_all * cap_up
     shape = jax.ShapeDtypeStruct
     scratch = pltpu.VMEM
     sem = pltpu.SemaphoreType.DMA
-    cell = cell_id.T
-    rank = slot_rank.T
-    disp = pl.pallas_call(
+    smalls = [
+        spacing.T, ray_length[None, :], targets, image_id[None, :],
+        code_table, table_first, table_second,
+    ]
+    inputs = [cell_id.T, slot_rank.T, features.transpose(1, 2, 0), params] + smalls
+    inputs = [pltpu.with_memory_space_constraint(value, pltpu.HBM) for value in inputs]
+    like = lambda value: shape(value.shape, value.dtype)
+    *placed, master = pl.pallas_call(
         functools.partial(place_kernel, groups, cap, cap_up),
-        out_shape=shape((groups, cap, LANES), BF16),
-        in_specs=[VMEM, VMEM, HBM],
-        out_specs=VMEM,
+        out_shape=[
+            shape((groups, cap, LANES), BF16), shape(params.shape, BF16),
+            like(inputs[0]), like(inputs[1]),
+        ] + [like(value) for value in smalls + [params]],
+        in_specs=[HBM] * len(inputs),
+        out_specs=[VMEM] * (5 + len(smalls)),
         scratch_shapes=[
             scratch((SAMPLES, ENC_WIDTH, ray_rows), BF16),
             scratch((sample_count, LANES), F32),
@@ -572,12 +611,12 @@
             scratch((experts_all, LANES), F32),
             scratch((SAMPLES, LANES), jnp.int32),
             pltpu.SMEM((SAMPLES, LANES), jnp.int32),
-            sem, sem,
+            sem((len(inputs),)), sem,
         ],
-        compiler_params=pltpu.CompilerParams(vmem_limit_bytes=48 * 2**20),
+        compiler_params=pltpu.CompilerParams(vmem_limit_bytes=12 * 2**20),
         cost_estimate=pl.CostEstimate(flops=0, bytes_accessed=6000 * sample_count, transcendentals=0),
         name="place",
-    )(cell, rank, features.transpose(1, 2, 0))
+    )(*inputs)
     all_rows = groups * cap
     grad_rows = params.shape[1]
     table_shape = shape(code_table.shape, F32)
@@ -587,12 +626,9 @@
         out_shape=(
             shape(params.shape, F32), shape((1, ray_rows), F32), table_shape, table_shape, table_shape,
         ),
-        in_specs=[VMEM, HBM] + [VMEM] * 9,
+        in_specs=[VMEM] * 11,
         out_specs=(VMEM,) * 5,
         scratch_shapes=[
-            scratch(params.shape, F32),
-            scratch((2, 16, NET_WIDTH), F32),
-            scratch(params.shape, BF16),
             scratch((2, LANES, NET_WIDTH), BF16),
             scratch((LAYERS - 1, 2, NET_WIDTH, NET_WIDTH), BF16),
             scratch((2, 8, NET_WIDTH), F32),
@@ -608,7 +644,7 @@
             scratch((8 * groups, LANES), F32),
             scratch((8 * SAMPLES, LANES), F32),
             scratch((SAMPLES, LANES), F32),
-            scratch((tiles * groups * 8, sample_count), BF16),
+            scratch((wide_rows, sample_count), BF16),
             scratch((LANES, sample_count), BF16),
             scratch((groups, 8, cap_up), BF16),
             scratch((groups, 8, cap_up), BF16),
@@ -621,25 +657,30 @@
             scratch((grad_rows, NET_WIDTH), BF16),
             scratch((grad_rows, NET_WIDTH), BF16),
             scratch((2, grad_rows, NET_WIDTH), F32),
-            sem((2,)),
             peers, peers, peers, peers, peers, peers, peers, peers, peers, peers,
             sem((3, LAYERS + 1)),
             sem((3, LAYERS + 1)),
         ],
         compiler_params=pltpu.CompilerParams(
-            collective_id=0, has_side_effects=True, vmem_limit_bytes=52 * 2**20
+            collective_id=0, has_side_effects=True, vmem_limit_bytes=36 * 2**20 + 2 * wide_rows * sample_count
         ),
         cost_estimate=pl.CostEstimate(flops=0, bytes_accessed=50000 * sample_count, transcendentals=0),
         name="step",
+    )(*placed)
+    whole = shape(params.shape, F32)
+    new_params, new_first, new_second, loss, *tables = pl.pallas_call(
+        update_kernel,
+        out_shape=[whole] * 3 + [shape((1, ray_rows), F32)] + [table_shape] * 3,
+        in_specs=[VMEM] * 8,
+        out_specs=[HBM] * 7,
+        scratch_shapes=[scratch(params.shape, F32)] * 3 + [sem((3, 4)), sem((4,))],
+        compiler_params=pltpu.CompilerParams(vmem_limit_bytes=16 * 2**20),
+        name="update",
     )(
-        disp, params, cell, rank, spacing.T, ray_length[None, :], targets, image_id[None, :],
-        code_table, table_first, table_second,
-    )
-    new_params, new_first, new_second = adam_update(params, param_grad, first_moment, second_moment)
-    return (
-        loss.reshape(ray_rows), new_params, new_first, new_second,
+        param_grad, master, first_moment, second_moment, loss,
         new_table, new_table_first, new_table_second,
     )
+    return (loss.reshape(ray_rows), new_params, new_first, new_second, *tables)
 
 
 def solution(mesh):

time: 83 us -> 68.8 us (0.83)
  local copies, waits for them, and re-layouts: 11 us -> 0.01 us
  other arithmetic: 5.48 us -> 0 us
  Pallas kernels: 65 us -> 67.9 us
    unnamed x30 -> x4, local copies, waits for them, and re-layouts: 11 us -> 0.01 us
    sub x1 -> x0, other arithmetic: 5.48 us -> none  [adam_update(): return (param_now - update, new_one, new_two)]
    pallas_call x0 -> x1, Pallas kernels: none -> 2.8 us  [shards(): pl.pallas_call(update_kernel, out_shape=[whole] * 3 + [shape((1, ray_rows...]
    pallas_call x1, Pallas kernels: 3.49 us -> 4.66 us  [shards(): pl.pallas_call(functools.partial(place_kernel, groups, cap, cap_up), out_...]
    pallas_call x1, Pallas kernels: 61.6 us -> 60.5 us  [shards(): pl.pallas_call(functools.partial(step_kernel, groups, cap, cap_up), out_s...]
where the time goes in v2:
time: 68.8 us; the launch traced here: 68.6 us
  Pallas kernels  67.9 us (99%)
  between operations  0.69 us (1%)
    pallas_call x1, Pallas kernels, shards(): pl.pallas_call(functools.partial(step_kernel, groups, cap, cap_up), out_s...  60.5 us
    pallas_call x1, Pallas kernels, shards(): pl.pallas_call(functools.partial(place_kernel, groups, cap, cap_up), out_...  4.66 us
    pallas_call x1, Pallas kernels, shards(): pl.pallas_call(update_kernel, out_shape=[whole] * 3 + [shape((1, ray_rows...  2.8 us

profile of v2, /device:TPU:0, one launch (start us, length us, event | category | flops | bytes accessed | tf_op | source)
XLA Modules:
  0.0 68.6 jit_solution(15696257672437084819)
XLA Ops:
  0.6 0.0 copy-start
  0.6 0.0 copy-start.1
  0.7 4.7 %place.1 = (bf16[8,384,128]{2,1,0:T(8,128)(2,1)S(1)}, bf16[2,848,256]{2,1,0:T(8,128)(2,1)S(1)}, s32[32,128]{1,0:T(8,128)S(1)}, s32[32,128]{1,0:T(8,128)S(1)}, f3...) custom-call(s32[32,128]{1,0:T(8,128)} %bitcast.8, ...), custom_call_target="tpu_custom_call" | custom-call | bytes 24576000 | tf_op jit(solution)/shard_map/place/pallas_call | solution.py:599
  5.3 60.5 %step.1 = (f32[2,848,256]{2,1,0:T(8,128)S(1)}, f32[1,128]{1,0:T(1,128)S(1)}, f32[16,64]{1,0:T(8,128)S(1)}, f32[16,64]{1,0:T(8,128)S(1)}, f32[16,64]{1,0:T(8,128)S(1)}) custom-call(bf16[8,384,128]{2,1,0:T(8,128)(2,1)S(1)} %get-tuple-element.31.disp, bf16[2,848,256]{2,1,0:T(8,128)(2,1)S(1)} %get-tuple-element.32.wt, s32[32,128]{1,0:T(8,128)S(1)} %get-tuple-element.33.cell_ref, ...), custom_call_target="tpu_custom_call" | custom-call | bytes 204800000 | tf_op jit(solution)/shard_map/step/pallas_call | solution.py:624
  65.8 0.0 copy-done
  65.8 0.0 copy-done.1
  65.8 2.8 %update.1 = (f32[2,848,256]{2,1,0:T(8,128)}, f32[2,848,256]{2,1,0:T(8,128)}, f32[2,848,256]{2,1,0:T(8,128)}, f32[1,128]{1,0:T(1,128)}, f32[16,64]{1,0:T(8,128)}, /*index=5*/f32[16,64]{1,0:T(8,128)}, f32[16,64]{1,0:T(8,128)}) custom-call(f32[2,848,256]{2,1,0:T(8,128)S(1)} %get-tuple-element.42.refs_0_, f32[2,848,256]{2,1,0:T(8,128)S(1)} %get-tuple-element.43.refs_1_, ...), custom_call_target="tpu_custom_call" | custom-call | tf_op jit(solution)/shard_map/update/pallas_call | solution.py:671
Async XLA Ops:
  0.6 65.2 %copy-start = (f32[2,848,256]{2,1,0:T(8,128)S(1)}, f32[2,848,256]{2,1,0:T(8,128)}, u32[]{:S(2)}) copy-start(f32[2,848,256]{2,1,0:T(8,128)} %refs_2_.3) | copy-start | bytes 5210116
  0.6 65.2 %copy-start.1 = (f32[2,848,256]{2,1,0:T(8,128)S(1)}, f32[2,848,256]{2,1,0:T(8,128)}, u32[]{:S(2)}) copy-start(f32[2,848,256]{2,1,0:T(8,128)} %refs_3_.1) | copy-start | bytes 5210116

commit v3 on v2

--- a/solution.py
+++ b/solution.py
@@ -1,4 +1,5 @@
 import functools
+import math
 
 import jax
 import jax.numpy as jnp
@@ -166,14 +167,14 @@
     disp, wt, cell_ref, rank_ref, spacing_ref, length_ref, target_ref, image_ref,
     code_ref, first_ref, second_ref,
     grad_out, loss_out, code_out, first_out, second_out,
-    m0, turned, head, recv, act, pre,
+    m0, turned, head, recv, act, act_t, feat_t, pre,
     raw_msg, back, tail_msg, tails, queries, shift, mix, eight, keys, wide, spots,
     cot_msg, cot_in, code_msg, code_in, cot_sum, bias, grad, half_in, sum_out, sum_in, full,
     s_out, r_out, s_back, r_back, s_tail, r_tail, s_cot, r_cot, s_code, r_code,
     s_sum, r_sum,
 ):
     tiles = cap_up // LANES
-    half = max(groups // 2 - 1, 0)
+    batch = LANES // math.gcd(cap, LANES)
     me = lax.axis_index("expert")
     my_dp = lax.axis_index("dp")
     core = lax.rem(my_dp, 2)
@@ -192,7 +193,7 @@
         pl.semaphore_signal(barrier, 1, device_id={"dp": peer}, device_id_type=MESH)
 
     def turn_of(j):
-        return lax.rem(j - 1 + half, groups - 1) + 1
+        return j
 
     def block_rows(k):
         return rows_of(k, cap, 16)
@@ -240,6 +241,11 @@
 
     m0[...] = jnp.zeros_like(m0)
     head[...] = jnp.zeros_like(head)
+    ones = jnp.ones((16, recv.shape[0]), BF16)
+    feat_t[LANES:, :] = ones
+    for layer in range(LAYERS - 1):
+        for h in range(2):
+            act_t[layer, h, NET_WIDTH:, :] = ones
     for h in range(2):
         m0[h, ENC_WIDTH * h : ENC_WIDTH * (h + 1), :] = wt[h, 0:ENC_WIDTH, :]
         head[h, 4 * h : 4 * h + 4, :] = tail_rows(wt, h).astype(F32)[0:4]
@@ -294,14 +300,31 @@
 
     lax.fori_loop(0, SAMPLES, spread, 0)
 
-    def step(j, carry):
-        k = turn_of(j)
+    def transpose(c):
+        rows = rows_of(c, batch * cap, 16)
+        lanes = pl.ds(pl.multiple_of(c * batch * cap, LANES), batch * cap)
+        feat_t[0:LANES, lanes] = recv[rows, :].T
+        for layer in range(LAYERS - 1):
+            for h in range(2):
+                act_t[layer, h, 0:NET_WIDTH, lanes] = act[layer, h, rows, :].T
+
+    def receive(k, carry):
         out_copy(k).wait_recv()
         process(k)
         back_copy(k).start()
         return carry
 
-    lax.fori_loop(1, groups, step, 0)
+    def receive_batch(c, carry):
+        if batch == 1:
+            receive(c, carry)
+        else:
+            lax.fori_loop(c * batch, (c + 1) * batch, receive, 0)
+        transpose(c)
+        return carry
+
+    lax.fori_loop(1, batch, receive, 0)
+    transpose(0)
+    lax.fori_loop(1, groups // batch, receive_batch, 0)
 
     each(lambda k: tail_copy(k).wait_recv())
 
@@ -454,13 +477,11 @@
 
     top = LAYERS - 1
     heads_bf = [head[h].astype(BF16) for h in range(2)]
-    bias[...] = jnp.zeros_like(bias)
     cot_sum[...] = jnp.zeros_like(cot_sum)
 
     def mask_store(layer, h, block, up):
-        value = jnp.where(act[layer, h, block, :].astype(F32) > 0, up, 0.0).astype(BF16)
-        pre[layer, h, block, :] = value
-        bias[layer, h] += jnp.sum(value.astype(F32).reshape(-1, 8, NET_WIDTH), axis=0)
+        up = up.astype(BF16)
+        pre[layer, h, block, :] = jnp.where(act[layer, h, block, :] > 0, up, jnp.zeros_like(up))
 
     def first_back(k, carry):
         block = block_rows(k)
@@ -495,16 +516,22 @@
                     )
                 return carry
 
-            lax.fori_loop(0, pieces, onward, 0)
-        for h in range(2):
-            if layer == 0:
-                value = dot(recv[...], pre[0, h], TN)
+            lax.fori_loop(0, pieces // 2, onward, 0)
+            second_stage(layer + 1)
+            lax.fori_loop(pieces // 2, pieces, onward, 0)
+        if layer == 0:
+            for h in range(2):
+                value = dot(feat_t[...], pre[0, h])
+                bias[0, h, 0:1, :] = value[LANES : LANES + 1]
                 grad[h, 0:ENC_WIDTH, :] = value[ENC_WIDTH * h : ENC_WIDTH * (h + 1)]
-            else:
-                grad[h, chunks[layer], :] = dot(act[layer - 1, h], pre[layer, h], TN)
-        near_copy(layer).start()
-        if layer < top:
-            second_stage(layer + 1)
+            near_copy(0).start()
+        else:
+            for h in (1 - core, core):
+                value = dot(act_t[layer - 1, h], pre[layer, h])
+                bias[layer, h, 0:1, :] = value[NET_WIDTH : NET_WIDTH + 1]
+                grad[h, chunks[layer], :] = value[0:NET_WIDTH]
+                if h is not core:
+                    near_copy(layer).start()
         if layer < top - 1:
             third_stage(layer + 2)
 
@@ -523,14 +550,14 @@
         line = jnp.concatenate([line, jnp.zeros((1, NET_WIDTH - LANES), F32)], axis=1)
         grad[h, HEAD_ROW : HEAD_ROW + 16, :] = jnp.concatenate(
             [hidden[h][4 * h : 4 * h + 4], codes[4 * h : 4 * h + 4], line]
-            + [jnp.sum(bias[layer, h], axis=0, keepdims=True) for layer in range(LAYERS)]
+            + [bias[layer, h, 0:1, :] for layer in range(LAYERS)]
             + [jnp.zeros((7 - LAYERS, NET_WIDTH), F32)],
             axis=0,
         )
     near_copy(LAYERS).start()
     second_stage(0)
+    second_stage(LAYERS)
     third_stage(1)
-    second_stage(LAYERS)
     third_stage(0)
     third_stage(LAYERS)
 
@@ -634,6 +661,8 @@
             scratch((2, 8, NET_WIDTH), F32),
             scratch((all_rows, LANES), BF16),
             scratch((LAYERS, 2, all_rows, NET_WIDTH), BF16),
+            scratch((LAYERS - 1, 2, NET_WIDTH + 16, all_rows), BF16),
+            scratch((LANES + 16, all_rows), BF16),
             scratch((LAYERS, 2, all_rows, NET_WIDTH), BF16),
             scratch((groups, 8, cap_up), F32),
             scratch((groups, 8, cap_up), F32),
@@ -662,7 +691,7 @@
             sem((3, LAYERS + 1)),
         ],
         compiler_params=pltpu.CompilerParams(
-            collective_id=0, has_side_effects=True, vmem_limit_bytes=36 * 2**20 + 2 * wide_rows * sample_count
+            collective_id=0, has_side_effects=True, vmem_limit_bytes=189 * 2**18 + 2 * wide_rows * sample_count
         ),
         cost_estimate=pl.CostEstimate(flops=0, bytes_accessed=50000 * sample_count, transcendentals=0),
         name="step",

time: 68.8 us -> 63 us (0.916)
  Pallas kernels: 67.9 us -> 62.1 us
    pallas_call x1, Pallas kernels: 60.5 us -> 54.7 us  [shards(): pl.pallas_call(functools.partial(step_kernel, groups, cap, cap_up), out_s...]
where the time goes in v3:
time: 63 us; the launch traced here: 62.8 us
  Pallas kernels  62.1 us (99%)
  between operations  0.69 us (1%)
    pallas_call x1, Pallas kernels, shards(): pl.pallas_call(functools.partial(step_kernel, groups, cap, cap_up), out_s...  54.7 us
    pallas_call x1, Pallas kernels, shards(): pl.pallas_call(functools.partial(place_kernel, groups, cap, cap_up), out_...  4.66 us
    pallas_call x1, Pallas kernels, shards(): pl.pallas_call(update_kernel, out_shape=[whole] * 3 + [shape((1, ray_rows...  2.8 us

profile of v3, /device:TPU:0, one launch (start us, length us, event | category | flops | bytes accessed | tf_op | source)
XLA Modules:
  0.0 62.8 jit_solution(12110000125966639874)
XLA Ops:
  0.6 0.0 copy-start
  0.6 0.0 copy-start.1
  0.7 4.7 %place.1 = (bf16[8,384,128]{2,1,0:T(8,128)(2,1)S(1)}, bf16[2,848,256]{2,1,0:T(8,128)(2,1)S(1)}, s32[32,128]{1,0:T(8,128)S(1)}, s32[32,128]{1,0:T(8,128)S(1)}, f3...) custom-call(s32[32,128]{1,0:T(8,128)} %bitcast.8, ...), custom_call_target="tpu_custom_call" | custom-call | bytes 24576000 | tf_op jit(solution)/shard_map/place/pallas_call | solution.py:626
  5.3 54.7 %step.1 = (f32[2,848,256]{2,1,0:T(8,128)S(1)}, f32[1,128]{1,0:T(1,128)S(1)}, f32[16,64]{1,0:T(8,128)S(1)}, f32[16,64]{1,0:T(8,128)S(1)}, f32[16,64]{1,0:T(8,128)S(1)}) custom-call(bf16[8,384,128]{2,1,0:T(8,128)(2,1)S(1)} %get-tuple-element.31.disp, bf16[2,848,256]{2,1,0:T(8,128)(2,1)S(1)} %get-tuple-element.32.wt, s32[32,128]{1,0:T(8,128)S(1)} %get-tuple-element.33.cell_ref, ...), custom_call_target="tpu_custom_call" | custom-call | bytes 204800000 | tf_op jit(solution)/shard_map/step/pallas_call | solution.py:651
  60.0 0.0 copy-done
  60.0 0.0 copy-done.1
  60.0 2.8 %update.1 = (f32[2,848,256]{2,1,0:T(8,128)}, f32[2,848,256]{2,1,0:T(8,128)}, f32[2,848,256]{2,1,0:T(8,128)}, f32[1,128]{1,0:T(1,128)}, f32[16,64]{1,0:T(8,128)}, /*index=5*/f32[16,64]{1,0:T(8,128)}, f32[16,64]{1,0:T(8,128)}) custom-call(f32[2,848,256]{2,1,0:T(8,128)S(1)} %get-tuple-element.42.refs_0_, f32[2,848,256]{2,1,0:T(8,128)S(1)} %get-tuple-element.43.refs_1_, ...), custom_call_target="tpu_custom_call" | custom-call | tf_op jit(solution)/shard_map/update/pallas_call | solution.py:700
Async XLA Ops:
  0.6 59.4 %copy-start = (f32[2,848,256]{2,1,0:T(8,128)S(1)}, f32[2,848,256]{2,1,0:T(8,128)}, u32[]{:S(2)}) copy-start(f32[2,848,256]{2,1,0:T(8,128)} %refs_2_.3) | copy-start | bytes 5210116
  0.6 59.4 %copy-start.1 = (f32[2,848,256]{2,1,0:T(8,128)S(1)}, f32[2,848,256]{2,1,0:T(8,128)}, u32[]{:S(2)}) copy-start(f32[2,848,256]{2,1,0:T(8,128)} %refs_3_.1) | copy-start | bytes 5210116

commit v4 on v3

--- a/solution.py
+++ b/solution.py
@@ -63,12 +63,12 @@
 def place_kernel(
     groups, cap, cap_up, cell_hbm, rank_hbm, feat_hbm, params_hbm, *refs,
 ):
-    smalls = refs[:7]
-    out_ref, wt, cell_ref, rank_ref = refs[7:11]
-    small_outs = refs[11:18]
-    master, feat, rows, table, counts, slot_vec, slot, load_sems, slot_sem = refs[18:]
+    others = refs[:9]
+    out_ref, master, cell_ref, rank_ref = refs[9:13]
+    other_outs = refs[13:22]
+    feat, rows, table, counts, slot_vec, slot, load_sems, slot_sem = refs[22:]
     pairs = [(cell_hbm, cell_ref), (rank_hbm, rank_ref), (feat_hbm, feat), (params_hbm, master)]
-    pairs += list(zip(smalls, small_outs))
+    pairs += list(zip(others, other_outs))
     loads = [
         pltpu.make_async_copy(source, target, load_sems.at[n])
         for n, (source, target) in enumerate(pairs)
@@ -127,7 +127,6 @@
     lax.fori_loop(0, groups, pack, 0)
     for load in loads[3:]:
         load.wait()
-    wt[...] = master[...].astype(BF16)
 
 
 def flipped(me, k, groups):
@@ -164,17 +163,18 @@
 
 def step_kernel(
     groups, cap, cap_up,
-    disp, wt, cell_ref, rank_ref, spacing_ref, length_ref, target_ref, image_ref,
-    code_ref, first_ref, second_ref,
-    grad_out, loss_out, code_out, first_out, second_out,
-    m0, turned, head, recv, act, act_t, feat_t, pre,
-    raw_msg, back, tail_msg, tails, queries, shift, mix, eight, keys, wide, spots,
-    cot_msg, cot_in, code_msg, code_in, cot_sum, bias, grad, half_in, sum_out, sum_in, full,
+    disp, master, cell_ref, rank_ref, spacing_ref, length_ref, target_ref, image_ref,
+    code_ref, first_ref, second_ref, moment_one, moment_two,
+    params_out, one_out, two_out, loss_out, code_out, first_out, second_out,
+    wt, m0, turned, head, recv, act, act_t, feat_t, pre,
+    raw_msg, back, tail_msg, tails, queries, shift, mix, eight, keys, spots,
+    cot_msg, cot_in, code_msg, code_in, cot_sum, bias, wide_grad, grad, half_out, half_in, sum_out, sum_in, full,
     s_out, r_out, s_back, r_back, s_tail, r_tail, s_cot, r_cot, s_code, r_code,
     s_sum, r_sum,
 ):
     tiles = cap_up // LANES
     batch = LANES // math.gcd(cap, LANES)
+    parts = [(0, cap)]
     me = lax.axis_index("expert")
     my_dp = lax.axis_index("dp")
     core = lax.rem(my_dp, 2)
@@ -204,8 +204,17 @@
             device_id={"expert": flipped(me, k, groups)}, device_id_type=MESH,
         )
 
-    def out_copy(k):
-        return peer_copy(k, disp.at[flipped(me, k, groups)], recv.at[block_rows(k)], s_out, r_out)
+    def part_rows(k, part):
+        start, size = parts[part]
+        return pl.ds(pl.multiple_of(k * cap + start, 16), size)
+
+    def out_copy(k, part):
+        start, size = parts[part]
+        return pltpu.make_async_remote_copy(
+            disp.at[flipped(me, k, groups), pl.ds(start, size)], recv.at[part_rows(k, part)],
+            s_out.at[part, k], r_out.at[part, k],
+            device_id={"expert": flipped(me, k, groups)}, device_id_type=MESH,
+        )
 
     def back_copy(k):
         return peer_copy(k, raw_msg.at[k], back.at[me], s_back, r_back)
@@ -229,7 +238,7 @@
     spot = iota((4, LANES), 0) == iota((4, LANES), 1)
     lane = iota((4, LANES), 1)
     for h in range(2):
-        tail = tail_rows(wt, h).astype(F32)
+        tail = tail_rows(master, h).astype(BF16).astype(F32)
         column = jnp.sum(jnp.where(spot, tail[8:9, 0:LANES], 0.0), axis=1, keepdims=True)
         tail_msg[4 * h : 4 * h + 4, :] = jnp.where(
             lane < CODE_WIDTH, tail[4:8, 0:LANES], jnp.where(lane == CODE_WIDTH, column, 0.0)
@@ -237,8 +246,13 @@
     tails[me] = tail_msg[...]
     pl.semaphore_wait(barrier, groups + 1)
     each(lambda k: tail_copy(k).start())
-    each(lambda k: out_copy(k).start())
-
+    def send(k):
+        for part in range(len(parts)):
+            out_copy(k, part).start()
+
+    each(send)
+    recv[block_rows(0), :] = disp[me]
+    wt[...] = master[...].astype(BF16)
     m0[...] = jnp.zeros_like(m0)
     head[...] = jnp.zeros_like(head)
     ones = jnp.ones((16, recv.shape[0]), BF16)
@@ -249,10 +263,10 @@
     for h in range(2):
         m0[h, ENC_WIDTH * h : ENC_WIDTH * (h + 1), :] = wt[h, 0:ENC_WIDTH, :]
         head[h, 4 * h : 4 * h + 4, :] = tail_rows(wt, h).astype(F32)[0:4]
-    recv[block_rows(0), :] = disp[me]
-
-    def process(k):
-        block = block_rows(k)
+
+    def process(k, part):
+        start, size = parts[part]
+        block = part_rows(k, part)
         features = recv[block, :]
         biases = [tail_rows(wt, h).astype(F32) for h in range(2)]
         current = [features, features]
@@ -264,9 +278,10 @@
                 act[layer, h, block, :] = current[h]
         for h in range(2):
             raw = dot(tail_rows(wt, h), current[h], NT)
-            raw_msg[k, 4 * h : 4 * h + 4, 0:cap] = raw[0:4]
-
-    process(0)
+            raw_msg[k, 4 * h : 4 * h + 4, start : start + size] = raw[0:4]
+
+    for part in range(len(parts)):
+        process(0, part)
     back[me] = raw_msg[0]
 
     for h in range(2):
@@ -309,22 +324,41 @@
                 act_t[layer, h, 0:NET_WIDTH, lanes] = act[layer, h, rows, :].T
 
     def receive(k, carry):
-        out_copy(k).wait_recv()
-        process(k)
+        for part in range(len(parts)):
+            out_copy(k, part).wait_recv()
+            process(k, part)
         back_copy(k).start()
         return carry
 
     def receive_batch(c, carry):
-        if batch == 1:
-            receive(c, carry)
-        else:
-            lax.fori_loop(c * batch, (c + 1) * batch, receive, 0)
+        lax.fori_loop(c * batch, (c + 1) * batch, receive, 0)
         transpose(c)
         return carry
 
-    lax.fori_loop(1, batch, receive, 0)
-    transpose(0)
-    lax.fori_loop(1, groups // batch, receive_batch, 0)
+    def receive_pair(pair, carry):
+        for part in range(len(parts)):
+
+            def arrive(k, inner):
+                out_copy(k, part).wait_recv()
+                process(k, part)
+                if part == len(parts) - 1:
+                    back_copy(k).start()
+                return inner
+
+            lax.fori_loop(2 * pair, 2 * pair + 2, arrive, 0)
+        transpose(2 * pair)
+        transpose(2 * pair + 1)
+        return carry
+
+    if batch == 1:
+        transpose(0)
+        receive(1, 0)
+        transpose(1)
+        lax.fori_loop(1, groups // 2, receive_pair, 0)
+    else:
+        lax.fori_loop(1, batch, receive, 0)
+        transpose(0)
+        lax.fori_loop(1, groups // batch, receive_batch, 0)
 
     each(lambda k: tail_copy(k).wait_recv())
 
@@ -400,26 +434,39 @@
     mix[...] = jnp.zeros_like(mix)
     member = lax.div(iota((8, LANES), 0), 4) * tiles
 
-    def widen(i, carry):
-        value = eight[rows_of(i, 8), :]
-        line = jnp.broadcast_to(keys[pl.ds(i, 1), :], (8, LANES))
+    wide_rows = tiles * groups * 8
+    strips = SAMPLES // 2
+
+    def widen(index, carry):
         sums = [0.0] * groups
-        for t in range(tiles):
-            for pair in range(groups // 2):
-                both = []
-                for g in (2 * pair, 2 * pair + 1):
-                    want = (member + (2 * g * tiles + t)).astype(F32)
-                    chosen = jnp.where(line == want, value, 0.0)
-                    sums[g] = sums[g] + chosen
-                    both.append(chosen)
-                start = (t * groups + 2 * pair) * 8
-                wide[start : start + 16, lane_block(i)] = jnp.concatenate(both, axis=0).astype(BF16)
+        for n in range(2):
+            i = 2 * index + n
+            value = eight[rows_of(i, 8), :]
+            line = jnp.broadcast_to(keys[pl.ds(i, 1), :], (8, LANES))
+            for t in range(tiles):
+                for pair in range(groups // 2):
+                    both = []
+                    for g in (2 * pair, 2 * pair + 1):
+                        want = (member + (2 * g * tiles + t)).astype(F32)
+                        chosen = jnp.where(line == want, value, 0.0)
+                        sums[g] = sums[g] + chosen
+                        both.append(chosen)
+                    start = index * wide_rows + (t * groups + 2 * pair) * 8
+                    pre[pl.ds(pl.multiple_of(start, 16), 16), n * LANES : (n + 1) * LANES] = (
+                        jnp.concatenate(both, axis=0).astype(BF16)
+                    )
         for g in range(groups):
             mix[8 * g : 8 * g + 8, :] += sums[g]
         return carry
 
-    lax.fori_loop(0, SAMPLES, widen, 0)
-    slots = dot(wide[...], spots[...], NT)
+    lax.fori_loop(0, strips, widen, 0)
+    slots = sum(
+        dot(
+            pre[n * wide_rows : (n + 1) * wide_rows, :],
+            spots[:, 2 * n * LANES : 2 * (n + 1) * LANES], NT,
+        )
+        for n in range(strips)
+    )
     for t in range(tiles):
         for g in range(groups):
             start = (t * groups + g) * 8
@@ -442,12 +489,17 @@
     first_out[...] = new_first
     second_out[...] = new_second
 
-    starts = [0] + [ENC_WIDTH + layer * NET_WIDTH for layer in range(LAYERS)] + [HEAD_ROW + 16]
-    chunks = [pl.ds(starts[j], starts[j + 1] - starts[j]) for j in range(LAYERS + 1)]
+    piece_rows = NET_WIDTH // 2
+    starts = [0] + list(range(ENC_WIDTH, HEAD_ROW + 1, piece_rows)) + [HEAD_ROW + 16]
+    chunks = [pl.ds(starts[j], starts[j + 1] - starts[j]) for j in range(len(starts) - 1)]
+    tail_chunk = len(chunks) - 1
+
+    def chunks_of(layer):
+        return [0] if layer == 0 else [2 * layer - 1, 2 * layer]
 
     def near_copy(j):
         return pltpu.make_async_remote_copy(
-            grad.at[1 - core, chunks[j]], half_in.at[chunks[j]],
+            half_out.at[chunks[j]], half_in.at[chunks[j]],
             s_sum.at[0, j], r_sum.at[0, j], device_id={"dp": near}, device_id_type=MESH,
         )
 
@@ -466,29 +518,39 @@
     def second_stage(j):
         near_copy(j).wait_recv()
         rows = chunks[j]
-        sum_out[rows, :] = (grad[core, rows, :] + half_in[rows, :]).astype(BF16)
+        sum_out[rows, :] = (grad[rows, :] + half_in[rows, :].astype(F32)).astype(BF16)
         far_copy(j).start()
 
     def third_stage(j):
         far_copy(j).wait_recv()
         rows = chunks[j]
-        full[core, rows, :] = sum_out[rows, :].astype(F32) + sum_in[rows, :].astype(F32)
+        total = sum_out[rows, :].astype(F32) + sum_in[rows, :].astype(F32)
+        full[core, rows, :] = total.astype(BF16)
         full_copy(j, core).start()
 
     top = LAYERS - 1
     heads_bf = [head[h].astype(BF16) for h in range(2)]
     cot_sum[...] = jnp.zeros_like(cot_sum)
 
-    def mask_store(layer, h, block, up):
+    all_rows = recv.shape[0]
+
+    def pre_rows(layer, h, start=0, size=all_rows):
+        first = (layer % 2 * 2 + h) * all_rows + start
+        return pl.ds(pl.multiple_of(first, 16), size)
+
+    def mask_store(layer, h, start, size, up):
         up = up.astype(BF16)
-        pre[layer, h, block, :] = jnp.where(act[layer, h, block, :] > 0, up, jnp.zeros_like(up))
+        rows = pl.ds(pl.multiple_of(start, 16), size)
+        pre[pre_rows(layer, h, start, size), :] = jnp.where(
+            act[layer, h, rows, :] > 0, up, jnp.zeros_like(up)
+        )
 
     def first_back(k, carry):
         block = block_rows(k)
         cot = cot_in[k, :, 0:cap]
         sums = []
         for h in range(2):
-            mask_store(top, h, block, dot(cot, heads_bf[h], TN))
+            mask_store(top, h, k * cap, cap, dot(cot, heads_bf[h], TN))
             sums.append(carry[h] + dot(cot, act[top, h, block, :]))
         cot_sum[...] += jnp.broadcast_to(
             jnp.sum(cot.astype(F32), axis=1, keepdims=True), (8, LANES)
@@ -503,37 +565,37 @@
     zeros = jnp.zeros((8, NET_WIDTH), F32)
     hidden = lax.fori_loop(1, groups, next_back, first_back(0, (zeros, zeros)))
 
-    pieces = 4
-    size = recv.shape[0] // pieces
     for layer in reversed(range(LAYERS)):
         if layer < top:
-
-            def onward(index, carry):
-                block = rows_of(index, size, 16)
-                for h in range(2):
-                    mask_store(
-                        layer, h, block, dot(pre[layer + 1, h, block, :], turned[layer, h])
-                    )
-                return carry
-
-            lax.fori_loop(0, pieces // 2, onward, 0)
-            second_stage(layer + 1)
-            lax.fori_loop(pieces // 2, pieces, onward, 0)
+            for h in range(2):
+                if h == 1:
+                    for j in chunks_of(layer + 1):
+                        second_stage(j)
+                up = dot(pre[pre_rows(layer + 1, h), :], turned[layer, h])
+                mask_store(layer, h, 0, all_rows, up)
+
         if layer == 0:
             for h in range(2):
-                value = dot(feat_t[...], pre[0, h])
+                value = dot(feat_t[...], pre[pre_rows(0, h), :])
                 bias[0, h, 0:1, :] = value[LANES : LANES + 1]
-                grad[h, 0:ENC_WIDTH, :] = value[ENC_WIDTH * h : ENC_WIDTH * (h + 1)]
+                wide_grad[h] = value[ENC_WIDTH * h : ENC_WIDTH * (h + 1)]
+            half_out[0:ENC_WIDTH, :] = wide_grad[1 - core].astype(BF16)
             near_copy(0).start()
+            grad[0:ENC_WIDTH, :] = wide_grad[core]
         else:
+            rows = pl.ds(starts[2 * layer - 1], NET_WIDTH)
             for h in (1 - core, core):
-                value = dot(act_t[layer - 1, h], pre[layer, h])
+                value = dot(act_t[layer - 1, h], pre[pre_rows(layer, h), :])
                 bias[layer, h, 0:1, :] = value[NET_WIDTH : NET_WIDTH + 1]
-                grad[h, chunks[layer], :] = value[0:NET_WIDTH]
-                if h is not core:
-                    near_copy(layer).start()
+                if h is core:
+                    grad[rows, :] = value[0:NET_WIDTH]
+                else:
+                    half_out[rows, :] = value[0:NET_WIDTH].astype(BF16)
+                    for j in chunks_of(layer):
+                        near_copy(j).start()
         if layer < top - 1:
-            third_stage(layer + 2)
+            for j in chunks_of(layer + 2):
+                third_stage(j)
 
     def add_codes(k, carry):
         code_copy(k).wait_recv()
@@ -548,54 +610,63 @@
         line = cot_row if h == 0 else pltpu.roll(cot_row, LANES - 4, 1)
         line = jnp.where(lane < 4, line, 0.0)
         line = jnp.concatenate([line, jnp.zeros((1, NET_WIDTH - LANES), F32)], axis=1)
-        grad[h, HEAD_ROW : HEAD_ROW + 16, :] = jnp.concatenate(
+        wide_grad[h, 0:16, :] = jnp.concatenate(
             [hidden[h][4 * h : 4 * h + 4], codes[4 * h : 4 * h + 4], line]
             + [bias[layer, h, 0:1, :] for layer in range(LAYERS)]
             + [jnp.zeros((7 - LAYERS, NET_WIDTH), F32)],
             axis=0,
         )
-    near_copy(LAYERS).start()
+    def finish(j):
+        full_copy(j, 1 - core).wait_recv()
+        start = starts[j]
+
+        def update(index, carry):
+            spot = (slice(None), pl.ds(pl.multiple_of(start + index * 16, 16), 16), slice(None))
+            values = adam_update(master[spot], full[spot].astype(F32), moment_one[spot], moment_two[spot])
+            for target, value in zip((params_out, one_out, two_out), values):
+                target[spot] = value
+            return carry
+
+        lax.fori_loop(0, (starts[j + 1] - start) // 16, update, 0)
+
+    tail = chunks[tail_chunk]
+    half_out[tail, :] = wide_grad[1 - core, 0:16, :].astype(BF16)
+    near_copy(tail_chunk).start()
+    grad[tail, :] = wide_grad[core, 0:16, :]
     second_stage(0)
-    second_stage(LAYERS)
-    third_stage(1)
-    third_stage(0)
-    third_stage(LAYERS)
+    second_stage(tail_chunk)
+    late = [chunks_of(1)[0], chunks_of(1)[1], 0, tail_chunk]
+    early = [chunks_of(3), chunks_of(2)[0:1], chunks_of(2)[1:], []]
+    for n in range(4):
+        for j in early[n]:
+            finish(j)
+        third_stage(late[n])
+        if n > 1:
+            finish(late[n - 2])
+    finish(0)
+    finish(tail_chunk)
 
     def drain(k):
-        for copy in (tail_copy, out_copy, back_copy, cot_copy, code_copy):
+        for part in range(len(parts)):
+            out_copy(k, part).wait_send()
+        for copy in (tail_copy, back_copy, cot_copy, code_copy):
             copy(k).wait_send()
 
     each(drain)
-    for j in (3, 2, 1, 0, LAYERS):
+    for j in range(len(chunks)):
         near_copy(j).wait_send()
         far_copy(j).wait_send()
         full_copy(j, core).wait_send()
-        full_copy(j, 1 - core).wait_recv()
-        grad_out[:, chunks[j], :] = full[:, chunks[j], :]
-
-
-def update_kernel(*refs):
-    grad, params, first, second = refs[:4]
-    smalls, large_outs, small_outs = refs[4:8], refs[8:11], refs[11:15]
-    stages, large_sems, small_sems = refs[15:18], refs[18], refs[19]
+
+
+def store_kernel(*refs):
+    count = len(refs) // 2
+    sems = refs[2 * count]
     copies = [
-        pltpu.make_async_copy(source, target, small_sems.at[n])
-        for n, (source, target) in enumerate(zip(smalls, small_outs))
+        pltpu.make_async_copy(refs[n], refs[count + n], sems.at[n]) for n in range(count)
     ]
     for copy in copies:
         copy.start()
-    half = grad.shape[1] // 2
-    for part in range(4):
-        rows = pl.ds(part % 2 * half, half)
-        spot = (part // 2, rows, slice(None))
-        values = adam_update(params[spot], grad[spot], first[spot], second[spot])
-        for n in range(3):
-            stages[n][spot] = values[n]
-            copy = pltpu.make_async_copy(
-                stages[n].at[spot], large_outs[n].at[spot], large_sems.at[n, part]
-            )
-            copy.start()
-            copies.append(copy)
     for copy in copies:
         copy.wait()
 
@@ -611,26 +682,24 @@
     cap = 2 * (sample_count * 3 // 4 // experts_all)
     cap_up = -(-cap // LANES) * LANES
     tiles = cap_up // LANES
-    wide_rows = tiles * groups * 8
     slots_up = experts_all * cap_up
     shape = jax.ShapeDtypeStruct
     scratch = pltpu.VMEM
     sem = pltpu.SemaphoreType.DMA
     smalls = [
         spacing.T, ray_length[None, :], targets, image_id[None, :],
-        code_table, table_first, table_second,
+        code_table, table_first, table_second, first_moment, second_moment,
     ]
     inputs = [cell_id.T, slot_rank.T, features.transpose(1, 2, 0), params] + smalls
     inputs = [pltpu.with_memory_space_constraint(value, pltpu.HBM) for value in inputs]
     like = lambda value: shape(value.shape, value.dtype)
-    *placed, master = pl.pallas_call(
+    placed = pl.pallas_call(
         functools.partial(place_kernel, groups, cap, cap_up),
         out_shape=[
-            shape((groups, cap, LANES), BF16), shape(params.shape, BF16),
-            like(inputs[0]), like(inputs[1]),
-        ] + [like(value) for value in smalls + [params]],
+            shape((groups, cap, LANES), BF16),
+        ] + [like(value) for value in [params] + inputs[0:2] + smalls],
         in_specs=[HBM] * len(inputs),
-        out_specs=[VMEM] * (5 + len(smalls)),
+        out_specs=[VMEM] * (4 + len(smalls)),
         scratch_shapes=[
             scratch((SAMPLES, ENC_WIDTH, ray_rows), BF16),
             scratch((sample_count, LANES), F32),
@@ -648,14 +717,15 @@
     grad_rows = params.shape[1]
     table_shape = shape(code_table.shape, F32)
     peers = sem((groups,))
-    param_grad, loss, new_table, new_table_first, new_table_second = pl.pallas_call(
+    step_vmem = 81 * 2**19 + groups * 48 * 2**10
+    whole = shape(params.shape, F32)
+    results = pl.pallas_call(
         functools.partial(step_kernel, groups, cap, cap_up),
-        out_shape=(
-            shape(params.shape, F32), shape((1, ray_rows), F32), table_shape, table_shape, table_shape,
-        ),
-        in_specs=[VMEM] * 11,
-        out_specs=(VMEM,) * 5,
+        out_shape=[whole] * 3 + [shape((1, ray_rows), F32)] + [table_shape] * 3,
+        in_specs=[VMEM] * 13,
+        out_specs=[VMEM] * 7,
         scratch_shapes=[
+            scratch(params.shape, BF16),
             scratch((2, LANES, NET_WIDTH), BF16),
             scratch((LAYERS - 1, 2, NET_WIDTH, NET_WIDTH), BF16),
             scratch((2, 8, NET_WIDTH), F32),
@@ -663,7 +733,7 @@
             scratch((LAYERS, 2, all_rows, NET_WIDTH), BF16),
             scratch((LAYERS - 1, 2, NET_WIDTH + 16, all_rows), BF16),
             scratch((LANES + 16, all_rows), BF16),
-            scratch((LAYERS, 2, all_rows, NET_WIDTH), BF16),
+            scratch((4 * all_rows, NET_WIDTH), BF16),
             scratch((groups, 8, cap_up), F32),
             scratch((groups, 8, cap_up), F32),
             scratch((8, LANES), F32),
@@ -673,7 +743,6 @@
             scratch((8 * groups, LANES), F32),
             scratch((8 * SAMPLES, LANES), F32),
             scratch((SAMPLES, LANES), F32),
-            scratch((wide_rows, sample_count), BF16),
             scratch((LANES, sample_count), BF16),
             scratch((groups, 8, cap_up), BF16),
             scratch((groups, 8, cap_up), BF16),
@@ -681,34 +750,33 @@
             scratch((groups, 8, LANES), F32),
             scratch((8, LANES), F32),
             scratch((LAYERS, 2, 8, NET_WIDTH), F32),
-            scratch((2, grad_rows, NET_WIDTH), F32),
+            scratch((2, ENC_WIDTH, NET_WIDTH), F32),
             scratch((grad_rows, NET_WIDTH), F32),
             scratch((grad_rows, NET_WIDTH), BF16),
             scratch((grad_rows, NET_WIDTH), BF16),
-            scratch((2, grad_rows, NET_WIDTH), F32),
-            peers, peers, peers, peers, peers, peers, peers, peers, peers, peers,
-            sem((3, LAYERS + 1)),
-            sem((3, LAYERS + 1)),
+            scratch((grad_rows, NET_WIDTH), BF16),
+            scratch((grad_rows, NET_WIDTH), BF16),
+            scratch((2, grad_rows, NET_WIDTH), BF16),
+            sem((2, groups)), sem((2, groups)),
+            peers, peers, peers, peers, peers, peers, peers, peers,
+            sem((3, 2 * LAYERS)),
+            sem((3, 2 * LAYERS)),
         ],
         compiler_params=pltpu.CompilerParams(
-            collective_id=0, has_side_effects=True, vmem_limit_bytes=189 * 2**18 + 2 * wide_rows * sample_count
+            collective_id=0, has_side_effects=True, vmem_limit_bytes=step_vmem
         ),
         cost_estimate=pl.CostEstimate(flops=0, bytes_accessed=50000 * sample_count, transcendentals=0),
         name="step",
     )(*placed)
-    whole = shape(params.shape, F32)
     new_params, new_first, new_second, loss, *tables = pl.pallas_call(
-        update_kernel,
-        out_shape=[whole] * 3 + [shape((1, ray_rows), F32)] + [table_shape] * 3,
-        in_specs=[VMEM] * 8,
+        store_kernel,
+        out_shape=[shape(value.shape, value.dtype) for value in results],
+        in_specs=[VMEM] * 7,
         out_specs=[HBM] * 7,
-        scratch_shapes=[scratch(params.shape, F32)] * 3 + [sem((3, 4)), sem((4,))],
-        compiler_params=pltpu.CompilerParams(vmem_limit_bytes=16 * 2**20),
-        name="update",
-    )(
-        param_grad, master, first_moment, second_moment, loss,
-        new_table, new_table_first, new_table_second,
-    )
+        scratch_shapes=[sem((7,))],
+        compiler_params=pltpu.CompilerParams(vmem_limit_bytes=2**20),
+        name="store",
+    )(*results)
     return (loss.reshape(ray_rows), new_params, new_first, new_second, *tables)
 
 

time: 63 us -> 62 us (0.984)
  Pallas kernels: 62.1 us -> 60.9 us
where the time goes in v4:
time: 62 us; the launch traced here: 61.8 us
  Pallas kernels  60.9 us (98%)
  between operations  0.81 us (1%)
    pallas_call x1, Pallas kernels, shards(): pl.pallas_call(functools.partial(step_kernel, groups, cap, cap_up), out_s...  54.1 us
    pallas_call x1, Pallas kernels, shards(): pl.pallas_call(functools.partial(place_kernel, groups, cap, cap_up), out_...  4.45 us
    pallas_call x1, Pallas kernels, shards(): pl.pallas_call(store_kernel, out_shape=[shape(value.shape, value.dtype) f...  2.41 us

profile of v4, /device:TPU:0, one launch (start us, length us, event | category | flops | bytes accessed | tf_op | source)
XLA Modules:
  0.0 61.8 jit_solution(15217233485883779665)
XLA Ops:
  0.6 4.5 %place.1 = (bf16[8,384,128]{2,1,0:T(8,128)(2,1)S(1)}, f32[2,848,256]{2,1,0:T(8,128)S(1)}, s32[32,128]{1,0:T(8,128)S(1)}, s32[32,128]{1,0:T(8,128)S(1)}, f32[32,1...) custom-call(s32[32,128]{1,0:T(8,128)} %bitcast.8, ...), custom_call_target="tpu_custom_call" | custom-call | bytes 24576000 | tf_op jit(solution)/shard_map/place/pallas_call | solution.py:696
  5.1 54.1 %step.1 = (f32[2,848,256]{2,1,0:T(8,128)S(1)}, f32[2,848,256]{2,1,0:T(8,128)S(1)}, f32[2,848,256]{2,1,0:T(8,128)S(1)}, f32[1,128]{1,0:T(1,128)S(1)}, f32[16,64]{...) custom-call(bf16[8,384,128]{2,1,0:T(8,128)(2,1)S(1)} %get-tuple-element.34.disp, ...), custom_call_target="tpu_custom_call" | custom-call | bytes 204800000 | tf_op jit(solution)/shard_map/step/pallas_call | solution.py:722
  59.2 2.4 %store.1 = (f32[2,848,256]{2,1,0:T(8,128)}, f32[2,848,256]{2,1,0:T(8,128)}, f32[2,848,256]{2,1,0:T(8,128)}, f32[1,128]{1,0:T(1,128)}, f32[16,64]{1,0:T(8,128)}, /*index=5*/f32[16,64]{1,0:T(8,128)}, f32[16,64]{1,0:T(8,128)}) custom-call(f32[2,848,256]{2,1,0:T(8,128)S(1)} %get-tuple-element.47.refs_0_, f32[2,848,256]{2,1,0:T(8,128)S(1)} %get-tuple-element.48.refs_1_, ...), custom_call_target="tpu_custom_call" | custom-call | tf_op jit(solution)/shard_map/store/pallas_call | solution.py:771
